TPU v7x, 512 devices: a whole 4x8x8 slice. The times are simulated.
512 devices in a mesh: group: 16 (over z, core), dom: 32 (over y, x).
Axes of the slice: x: 4, y: 8, z: 8, core: 2. Of those that a mesh axis runs over, the one named last changes fastest.
Arguments:
- adjoint: float32 [6, 524288], P(None, ('group', 'dom')), may hold values from -4 to 4
- gradient: float32 [6, 524288], P(None, ('group', 'dom')), may hold values from -6 to 6
- precond: float32 [6, 524288], P(None, ('group', 'dom')), may hold values from 0.3 to 1
- band: bfloat16 [5, 6, 6, 524288], P(None, None, None, ('group', 'dom')), may hold values from -0.75 to 0.75
- face_jac: bfloat16 [262144, 768], P(('group', 'dom')), may hold values from -2.5 to 2.5
- face_cell: int32 [262144], P(('group', 'dom')), may hold values from 0 to 32767, as said below
- face_box: int32 [262144, 1], P(('group', 'dom')), may hold values from 0 to 31; in each aligned block of 512 rows (0 to 511, 512 to 1023, ...) at most 64 rows name the same one
Outputs:
- adjoint_out: float32 [6, 524288], P(None, ('group', 'dom'))
- box_sens: float32 [512, 128], P(('group', 'dom'))
Inputs may be any that keep to these rules, and one draw needn't show every extreme that they name: `face_box`: within the rows of one device no box is named by more than 64 faces, a bound that some block reaches. `face_cell`: within the faces of one device no partition of 1024 cells (cells p * 1024 to (p + 1) * 1024 - 1) is read by more than 64 faces, and some partition by exactly 64.
All inputs are finite; a program needn't handle non-finite values.
Results may differ from a plain program's by a relative error of at most 0.0003.
Values sent between devices are 32-bit elements; how exact they have to be, the bound alone decides.
A program may use at most 64 MiB of HBM per device.

v0:
```python
import jax
import jax.numpy as jnp
from jax import lax
from jax.sharding import PartitionSpec as P

NVAR = 6
SENS = 128
BAND = 5
SWEEPS = 3


def padded_2(array, sides, width):
    for axis, dim in sides:
        size, length = (lax.axis_size(axis), array.shape[dim])
        up = [(i, (i + 1) % size) for i in range(size - 1)]
        down = [(j, i) for i, j in up]
        last = lax.slice_in_dim(array, length - width, length, axis=dim)
        first = lax.slice_in_dim(array, 0, width, axis=dim)
        before = lax.ppermute(last, axis, up)
        after = lax.ppermute(first, axis, down)
        array = jnp.concatenate([before, array, after], axis=dim)
    return array


def shards(adjoint, gradient, precond, band, face_jac, face_cell, face_box):
    cell_count = adjoint.shape[1]
    state_adj = adjoint
    for sweep_index in range(SWEEPS):
        padded = padded_2(state_adj, ((("group", "dom"), 1),), 2)
        band_sum = jnp.zeros(state_adj.shape, jnp.float32)
        for offset_k in range(BAND):
            shifted = padded[:, offset_k : offset_k + cell_count]
            band_sum = band_sum + jnp.sum(
                band[offset_k].astype(jnp.float32) * shifted[:, None, :], axis=0
            )
        state_adj = state_adj + precond * (gradient - band_sum)
    face_count = face_cell.shape[0]
    owners = lax.axis_size("dom")
    owner_ids = jnp.arange(owners, dtype=jnp.int32)
    gathered = lax.all_gather(state_adj, "dom", axis=1, tiled=True)
    face_psi = jnp.take(gathered, face_cell, axis=1)
    jacobian = face_jac.astype(jnp.float32).reshape(face_count, NVAR, SENS)
    rows = jnp.sum(face_psi.T[:, :, None] * jacobian, axis=1)
    target = face_box[:, 0]
    onehot = (target[:, None] == owner_ids[None, :]).astype(jnp.int32)
    partial_sums = jnp.dot(
        onehot.astype(jnp.float32).T,
        rows,
        precision=lax.Precision.HIGHEST,
        preferred_element_type=jnp.float32,
    )
    box_sens = lax.psum_scatter(partial_sums, "dom", scatter_dimension=0, tiled=True)
    return (state_adj, box_sens)


def solution(mesh):
    return jax.shard_map(
        shards,
        mesh=mesh,
        in_specs=(
            P(None, ("group", "dom")),
            P(None, ("group", "dom")),
            P(None, ("group", "dom")),
            P(None, None, None, ("group", "dom")),
            P(("group", "dom"), None),
            P(("group", "dom")),
            P(("group", "dom"), None),
        ),
        out_specs=(P(None, ("group", "dom")), P(("group", "dom"), None)),
        check_vma=False,
    )
```

profile of v0, /device:TPU:256, one launch (start us, length us, event | category | flops | bytes accessed | tf_op | source)
XLA Modules:
  0.0 247.5 jit_solution(16560376052622453711)
XLA Ops:
  0.6 0.0 copy-start.1
  0.6 0.0 copy-start
  0.7 0.0 copy-start.3
  0.7 0.0 copy-start.2
  0.7 0.8 fusion.28
  1.5 3.4 %collective-permute-start = (f32[6,2]{1,0:T(8,128)S(1)}, f32[6,2]{1,0:T(8,128)S(1)}, u32[]{:S(2)}, u32[]{:S(2)}) collective-permute-start(f32[6,2]{1,0:T(8,128)S(1)} %get-tuple-element.44), channel_id=1, source_target_pairs={{0,1},{1,2},{2,3},{3,4},{4,5},{5,6},{6,7},{7,8},{8,9},{9,10},{10,1... | collective-permute-start | bytes 152 | tf_op jit(solution)/shard_map/ppermute | solution.py:19
  4.9 7.6 %collective-permute-start.1 = (f32[6,2]{1,0:T(8,128)S(1)}, f32[6,2]{1,0:T(8,128)S(1)}, u32[]{:S(2)}, u32[]{:S(2)}) collective-permute-start(f32[6,2]{1,0:T(8,128)S(1)} %get-tuple-element.43), channel_id=1, source_target_pairs={{1,0},{2,1},{3,2},{4,3},{5,4},{6,5},{7,6},{8,7},{9,8},{10,9},{11,1... | collective-permute-start | bytes 152 | tf_op jit(solution)/shard_map/ppermute | solution.py:20
  12.5 0.7 compare_select_fusion
  13.2 0.7 compare_and_fusion
  13.9 1.4 copy.108
  15.3 1.3 dynamic-slice
  16.6 0.0 collective-permute-done
  16.6 0.0 copy-done.1
  16.6 0.1 fusion.24
  16.7 0.0 collective-permute-done.1
  16.7 0.1 fusion.25
  16.8 0.0 copy-done
  16.8 0.1 fusion.7
  16.9 0.0 copy-done.3
  16.9 0.0 copy-done.2
  17.0 0.1 fusion.27
  17.0 1.9 collective-permute-start.2
  18.9 9.1 %collective-permute-start.3 = (f32[6,2]{1,0:T(8,128)S(1)}, f32[6,2]{1,0:T(8,128)S(1)}, u32[]{:S(2)}, u32[]{:S(2)}) collective-permute-start(f32[6,2]{1,0:T(8,128)S(1)} %get-tuple-element.41), channel_id=1, source_target_pairs={{1,0},{2,1},{3,2},{4,3},{5,4},{6,5},{7,6},{8,7},{9,8},{10,9},{11,1... | collective-permute-start | bytes 152 | tf_op jit(solution)/shard_map/ppermute | solution.py:20
  28.0 0.0 collective-permute-done.2
  28.0 1.3 collective-permute-done.3
  29.3 0.1 pad_maximum_fusion.2
  29.4 0.1 fusion.8
  29.6 0.1 fusion.26
  29.7 1.9 collective-permute-start.4
  31.6 9.1 %collective-permute-start.5 = (f32[6,2]{1,0:T(8,128)S(1)}, f32[6,2]{1,0:T(8,128)S(1)}, u32[]{:S(2)}, u32[]{:S(2)}) collective-permute-start(f32[6,2]{1,0:T(8,128)S(1)} %get-tuple-element.37), channel_id=1, source_target_pairs={{1,0},{2,1},{3,2},{4,3},{5,4},{6,5},{7,6},{8,7},{9,8},{10,9},{11,1... | collective-permute-start | bytes 152 | tf_op jit(solution)/shard_map/ppermute | solution.py:20
  40.7 0.0 collective-permute-done.4
  40.7 1.3 collective-permute-done.5
  42.0 0.1 pad_maximum_fusion
  42.1 0.1 fusion.9
  42.3 0.0 copy-start.4
  42.3 47.0 %all_gather.3 = f32[6,32768]{1,0:T(8,128)S(1)} all-gather(f32[6,1024]{1,0:T(8,128)S(1)} %multiply_add_fusion), channel_id=1, replica_groups=mesh['group'=16,'dom'=32] {'dom'}, dimensions={1}, use_global_device_ids=true | all-gather | bytes 811008 | tf_op jit(solution)/shard_map/all_gather | solution.py:40
  89.3 9.0 %copy.106 = f32[6,32768]{0,1:T(8,128)} copy(f32[6,32768]{1,0:T(8,128)S(1)} %all_gather.3) | data formatting | bytes 1572864 | tf_op jit(solution)/shard_map/all_gather | solution.py:40
  98.3 0.0 copy-done.4
  98.3 0.0 copy-start.5
  98.3 6.8 %gather_fusion = f32[512,6]{1,0:T(8,128)S(1)} fusion(f32[6,32768]{0,1:T(8,128)} %copy.106, s32[1024]{0:T(1024)S(1)} %pad_clamp_fusion), kind=kCustom, calls=%fused_computation | custom fusion | bytes 26624 | tf_op jit(solution)/shard_map/jit(_take)/gather | solution.py:41
  105.1 0.1 broadcast_select_fusion
  105.3 0.1 copy.107
  105.4 0.2 fusion
  105.5 0.0 copy-done.5
  105.6 0.5 fusion.1
  106.1 140.3 %all-reduce = f32[32,128]{1,0:T(8,128)S(1)} all-reduce(f32[32,128]{1,0:T(8,128)S(1)} %fusion.1), channel_id=2, replica_groups=mesh['group'=16,'dom'=32] {'dom'}, use_global_device_ids=true, to_apply=%region_16.17.clone | all-reduce | flops 4096 | bytes 32768
  246.4 1.1 constant_dynamic-slice_fusion
  (5 shorter events, 0.1 us)
Async XLA Ops:
  0.6 15.9 %copy-start.1 = (f32[6,1024]{1,0:T(8,128)S(1)}, f32[6,1024]{1,0:T(8,128)}, u32[]{:S(2)}) copy-start(f32[6,1024]{1,0:T(8,128)} %param.7) | copy-start | bytes 73732
  0.6 16.1 %copy-start = (bf16[5,6,6,1024]{3,2,1,0:T(8,128)(2,1)S(1)}, bf16[5,6,6,1024]{3,2,1,0:T(8,128)(2,1)}, u32[]{:S(2)}) copy-start(bf16[5,6,6,1024]{3,2,1,0:T(8,128)(2,1)} %param.10) | copy-start | bytes 1105924
  0.7 16.3 %copy-start.3 = (f32[6,1024]{1,0:T(8,128)S(1)}, f32[6,1024]{1,0:T(8,128)}, u32[]{:S(2)}) copy-start(f32[6,1024]{1,0:T(8,128)} %param.8) | copy-start | bytes 73732
  0.7 16.3 %copy-start.2 = (f32[6,1024]{1,0:T(8,128)S(1)}, f32[6,1024]{1,0:T(8,128)}, u32[]{:S(2)}) copy-start(f32[6,1024]{1,0:T(8,128)} %param.9) | copy-start | bytes 73732
  1.5 15.1 %collective-permute-start = (f32[6,2]{1,0:T(8,128)S(1)}, f32[6,2]{1,0:T(8,128)S(1)}, u32[]{:S(2)}, u32[]{:S(2)}) collective-permute-start(f32[6,2]{1,0:T(8,128)S(1)} %get-tuple-element.44), channel_id=1, source_target_pairs={{0,1},{1,2},{2,3},{3,4},{4,5},{5,6},{6,7},{7,8},{8,9},{9,10},{10,1... | collective-permute-start | bytes 152 | tf_op jit(solution)/shard_map/ppermute | solution.py:19
  4.9 11.8 %collective-permute-start.1 = (f32[6,2]{1,0:T(8,128)S(1)}, f32[6,2]{1,0:T(8,128)S(1)}, u32[]{:S(2)}, u32[]{:S(2)}) collective-permute-start(f32[6,2]{1,0:T(8,128)S(1)} %get-tuple-element.43), channel_id=1, source_target_pairs={{1,0},{2,1},{3,2},{4,3},{5,4},{6,5},{7,6},{8,7},{9,8},{10,9},{11,1... | collective-permute-start | bytes 152 | tf_op jit(solution)/shard_map/ppermute | solution.py:20
  17.0 11.0 %collective-permute-start.2 = (f32[6,2]{1,0:T(8,128)S(1)}, f32[6,2]{1,0:T(8,128)S(1)}, u32[]{:S(2)}, u32[]{:S(2)}) collective-permute-start(f32[6,2]{1,0:T(8,128)S(1)} %get-tuple-element.42), channel_id=1, source_target_pairs={{0,1},{1,2},{2,3},{3,4},{4,5},{5,6},{6,7},{7,8},{8,9},{9,10},{10,1... | collective-permute-start | bytes 152 | tf_op jit(solution)/shard_map/ppermute | solution.py:19
  18.9 10.4 %collective-permute-start.3 = (f32[6,2]{1,0:T(8,128)S(1)}, f32[6,2]{1,0:T(8,128)S(1)}, u32[]{:S(2)}, u32[]{:S(2)}) collective-permute-start(f32[6,2]{1,0:T(8,128)S(1)} %get-tuple-element.41), channel_id=1, source_target_pairs={{1,0},{2,1},{3,2},{4,3},{5,4},{6,5},{7,6},{8,7},{9,8},{10,9},{11,1... | collective-permute-start | bytes 152 | tf_op jit(solution)/shard_map/ppermute | solution.py:20
  29.7 11.0 %collective-permute-start.4 = (f32[6,2]{1,0:T(8,128)S(1)}, f32[6,2]{1,0:T(8,128)S(1)}, u32[]{:S(2)}, u32[]{:S(2)}) collective-permute-start(f32[6,2]{1,0:T(8,128)S(1)} %get-tuple-element.38), channel_id=1, source_target_pairs={{0,1},{1,2},{2,3},{3,4},{4,5},{5,6},{6,7},{7,8},{8,9},{9,10},{10,1... | collective-permute-start | bytes 152 | tf_op jit(solution)/shard_map/ppermute | solution.py:19
  31.6 10.4 %collective-permute-start.5 = (f32[6,2]{1,0:T(8,128)S(1)}, f32[6,2]{1,0:T(8,128)S(1)}, u32[]{:S(2)}, u32[]{:S(2)}) collective-permute-start(f32[6,2]{1,0:T(8,128)S(1)} %get-tuple-element.37), channel_id=1, source_target_pairs={{1,0},{2,1},{3,2},{4,3},{5,4},{6,5},{7,6},{8,7},{9,8},{10,9},{11,1... | collective-permute-start | bytes 152 | tf_op jit(solution)/shard_map/ppermute | solution.py:20
  42.3 56.0 %copy-start.4 = (f32[6,1024]{1,0:T(8,128)}, f32[6,1024]{1,0:T(8,128)S(1)}, u32[]{:S(2)}) copy-start(f32[6,1024]{1,0:T(8,128)S(1)} %multiply_add_fusion) | copy-start | bytes 73732
  98.3 7.2 %copy-start.5 = (s32[512,1]{0,1:T(1,128)S(1)}, s32[512,1]{0,1:T(1,128)}, u32[]{:S(2)}) copy-start(s32[512,1]{0,1:T(1,128)} %param.13) | copy-start | bytes 6148
where the time goes:
time: 248 us; the launch traced here: 247 us
  blocking collectives  187 us (75%)
  starting transfers between devices  32.9 us (13%)
  local copies, waits for them, and re-layouts  20.8 us (8%)
  waiting for transfers between devices  2.6 us (1%)
    unnamed x1, blocking collectives  140 us
    all_gather x1, blocking collectives, shards(): gathered = lax.all_gather(state_adj, 'dom', axis=1, tiled=True)  47 us
    ppermute x3, starting transfers between devices, padded_2(): after = lax.ppermute(first, axis, down)  25.7 us
    all_gather x1, local copies, waits for them, and re-layouts, shards(): gathered = lax.all_gather(state_adj, 'dom', axis=1, tiled=True)  9 us
    ppermute x3, starting transfers between devices, padded_2(): before = lax.ppermute(last, axis, up)  7.21 us
    gather x1, local copies, waits for them, and re-layouts, shards(): face_psi = jnp.take(gathered, face_cell, axis=1)  6.81 us
  transfers between devices with their start and end apart: 6, of which 2 were waited for; matrix products, arithmetic and copies ran while one was open for 2% of the time, Pallas kernels for 0%

commit v1 on v0

v1 whole, which is shorter than its diff:
```python
import functools

import jax
import jax.numpy as jnp
from jax import lax
from jax.experimental import pallas as pl
from jax.experimental.pallas import tpu as pltpu
from jax.sharding import PartitionSpec as P

NVAR = 6
SENS = 128
BAND = 5
SWEEPS = 3
CAP = 64
LANES = 128
X, Y = 4, 8
MESH = pl.DeviceIdType.MESH

FAR_FIRST = sorted(
    range(1, X * Y),
    key=lambda s: -(min(s % X, X - s % X) + min(s // X, Y - s // X)),
)


def take_lanes(values, index):
    return jnp.take_along_axis(values, index, axis=1, mode="promise_in_bounds")


def kernel(
    groups,
    adj_h,
    grad_h,
    pre_h,
    band_h,
    jac_h,
    cell_h,
    box_h,
    adj_o,
    box_o,
    adj_v,
    grad_v,
    pre_v,
    band_v,
    jac_v,
    cell_v,
    box_v,
    bandf,
    shf,
    psi8,
    out_v,
    halo_s,
    halo_l,
    halo_r,
    req_s,
    req_r,
    resp_s,
    resp_r,
    part_s,
    part_r,
    sens_v,
    in_sem,
    halo_send,
    halo_recv,
    req_send,
    req_recv,
    resp_send,
    resp_recv,
    part_send,
    part_recv,
    out_sem,
):
    cells = adj_h.shape[1]
    faces = jac_h.shape[0]
    dom_count = X * Y
    blocks = cells // LANES
    ext = cells + LANES
    g = lax.axis_index("group")
    d = lax.axis_index("dom")
    y, x = d // X, d % X
    rows = [((y + dy) % Y) * X for dy in range(Y)]
    columns = [(x + dx) % X for dx in range(X)]
    back_rows = [((y + Y - dy) % Y) * X for dy in range(Y)]
    back_columns = [(x + X - dx) % X for dx in range(X)]
    ahead = [rows[s // X] + columns[s % X] for s in range(dom_count)]
    behind = [back_rows[s // X] + back_columns[s % X] for s in range(dom_count)]
    total = groups * dom_count
    place = g * dom_count + d
    after = (place + 1) % total
    before = (place + total - 1) % total
    after_id = (after // dom_count, after % dom_count)
    before_id = (before // dom_count, before % dom_count)

    barrier = pltpu.get_barrier_semaphore()
    for target in (before_id, after_id):
        pl.semaphore_signal(barrier, inc=1, device_id=target, device_id_type=MESH)
    for s in FAR_FIRST:
        pl.semaphore_signal(
            barrier, inc=1, device_id=(g, ahead[s]), device_id_type=MESH
        )

    loads = [
        pltpu.make_async_copy(src, dst, in_sem.at[i])
        for i, (src, dst) in enumerate(
            (
                (cell_h, cell_v),
                (band_h, band_v),
                (adj_h, adj_v),
                (grad_h, grad_v),
                (pre_h, pre_v),
                (box_h, box_v),
                (jac_h, jac_v),
            )
        )
    ]
    for load in loads:
        load.start()

    loads[0].wait()
    cell = cell_v[...]
    owner, local = cell // cells, cell % cells
    far = ((owner // X - y + Y) % Y) * X + (owner % X - x + X) % X
    slots = lax.broadcasted_iota(jnp.int32, (dom_count, faces), 0)
    reads = jnp.where(slots == far, 1.0, 0.0)
    earlier = lax.broadcasted_iota(jnp.int32, (faces, faces), 0)
    later = lax.broadcasted_iota(jnp.int32, (faces, faces), 1)
    upper = jnp.where(earlier < later, 1.0, 0.0).astype(jnp.bfloat16)
    reads_b = reads.astype(jnp.bfloat16)
    counts = jnp.dot(reads_b, upper, preferred_element_type=jnp.float32)
    rank = jnp.sum(reads * counts, axis=0, keepdims=True).astype(jnp.int32)
    lines = lax.broadcasted_iota(jnp.int32, (2 * CAP, faces), 0)
    wanted = jnp.where(
        lines < CAP, (local // LANES).astype(jnp.float32), (local % LANES).astype(jnp.float32)
    )
    wanted = jnp.where(lines % CAP == rank, wanted, 0.0).astype(jnp.bfloat16)
    requests = lax.dot_general(
        reads_b, wanted, (((1,), (1,)), ((), ())), preferred_element_type=jnp.float32
    ).astype(jnp.int32)
    for s in range(dom_count):
        req_s[s] = requests[s : s + 1]

    lane = lax.broadcasted_iota(jnp.int32, (NVAR, LANES), 1)
    head = lane < CAP
    loads[1].wait()
    half = BAND * NVAR // 2
    packed = [jnp.zeros((NVAR, LANES), jnp.float32)] * 2
    for t in range(BAND * NVAR):
        tile = band_v[t // NVAR, t % NVAR].astype(jnp.float32)
        bandf[t, :, :cells] = tile
        ends = jnp.where(head, tile[:, :LANES], tile[:, cells - LANES :])
        u = t % half
        ends = pltpu.roll(ends, 8 * u + 4, 1)
        packed[t // half] = jnp.where(lane // 8 == u, ends, packed[t // half])
    halo_s[0] = packed[0]
    halo_s[1] = packed[1]
    for load in loads[2:5]:
        load.wait()
    adj, grad, pre = adj_v[...], grad_v[...], pre_v[...]
    ends = [
        jnp.where(head, v[:, :LANES], v[:, cells - LANES :]) for v in (adj, grad, pre)
    ]
    near = (lane < 16) | (lane >= 112)
    halo_s[2] = jnp.where(
        near,
        ends[0],
        jnp.where(head, pltpu.roll(ends[1], 32, 1), pltpu.roll(ends[2], 80, 1)),
    )
    psi8[NVAR:, :] = jnp.zeros((8 - NVAR, cells), jnp.float32)

    pl.semaphore_wait(barrier, dom_count + 1)

    halo_copies = []
    for i, (target, landing) in enumerate(((after_id, halo_l), (before_id, halo_r))):
        halo_copies.append(
            pltpu.make_async_remote_copy(
                src_ref=halo_s,
                dst_ref=landing,
                send_sem=halo_send.at[i],
                recv_sem=halo_recv.at[i],
                device_id=target,
                device_id_type=MESH,
            )
        )
    for copy in halo_copies:
        copy.start()

    def send(source, landing, send_sem, recv_sem, s, target):
        pltpu.make_async_remote_copy(
            src_ref=source.at[s],
            dst_ref=landing.at[s],
            send_sem=send_sem,
            recv_sem=recv_sem,
            device_id=(g, target),
            device_id_type=MESH,
        ).start()

    def wait_all(ref, sem):
        all_slots = ref.at[pl.ds(1, dom_count - 1)]
        pltpu.make_async_copy(all_slots, all_slots, sem).wait()

    for s in FAR_FIRST:
        send(req_s, req_r, req_send, req_recv, s, ahead[s])

    rank8 = jnp.broadcast_to(rank, (8, faces))
    pick = rank8 + jnp.where(
        lax.broadcasted_iota(jnp.int32, (8, faces), 0) < 4, 0, CAP
    )
    far8 = jnp.broadcast_to(far, (8, faces))
    loads[5].wait()
    box = box_v[...]
    box_far = ((box // X - y + Y) % Y) * X + (box % X - x + X) % X
    feeds = slots == box_far

    for copy in halo_copies:
        copy.wait()
    first, last = place == 0, place == total - 1
    left = jnp.where(first, 0.0, halo_l[...])
    right = jnp.where(last, 0.0, halo_r[...])
    from_left = lane % 8 < 4
    for h in range(2):
        both = jnp.where(from_left, left[h], right[h])
        for u in range(half):
            bandf[h * half + u, :, cells:] = pltpu.roll(both, LANES - (8 * u + 4), 1)
    both_psi = jnp.where(head, right[2], left[2])
    left_grad, right_grad = pltpu.roll(left[2], 96, 1), pltpu.roll(right[2], 96, 1)
    left_pre, right_pre = pltpu.roll(left[2], 48, 1), pltpu.roll(right[2], 48, 1)
    both_grad = jnp.where(head, right_grad, left_grad)
    both_pre = jnp.where(head, right_pre, left_pre)
    psi = jnp.concatenate([adj, both_psi], axis=1)
    grad = jnp.concatenate([grad, both_grad], axis=1)
    pre = jnp.concatenate([pre, both_pre], axis=1)
    for sweep in range(SWEEPS):
        width = cells if sweep == SWEEPS - 1 else ext
        for k in range(BAND):
            shf[k] = psi if k == 2 else pltpu.roll(psi, (2 - k) % ext, 1)
        total_sum = None
        for t in range(BAND * NVAR):
            k, b = t // NVAR, t % NVAR
            column = jnp.broadcast_to(shf[k, b : b + 1, :width], (NVAR, width))
            term = bandf[t, :, :width] * column
            total_sum = term if total_sum is None else total_sum + term
        psi = psi[:, :width] + pre[:, :width] * (grad[:, :width] - total_sum)
    psi8[:NVAR, :] = psi
    out_v[...] = psi
    adj_copy = pltpu.make_async_copy(out_v, adj_o, out_sem.at[0])
    adj_copy.start()

    chunks = [psi8[:, c * LANES : (c + 1) * LANES] for c in range(blocks)]
    low8 = lax.broadcasted_iota(jnp.int32, (8, LANES), 1) < CAP

    def answer(s, wish):
        turned = pltpu.roll(wish, CAP, 1)
        low1 = low8[:1]
        chunk = jnp.broadcast_to(jnp.where(low1, wish, turned), (8, LANES))
        place_in = jnp.broadcast_to(jnp.where(low1, turned, wish), (8, LANES))
        found = take_lanes(chunks[0], place_in)
        for c in range(1, blocks):
            found = jnp.where(chunk == c, take_lanes(chunks[c], place_in), found)
        both = jnp.where(low8, found, pltpu.roll(found, 5, 0))
        return both[:4]

    resp_r[0] = answer(0, req_s[0])
    wait_all(req_r, req_recv)
    step = 4
    for start in range(0, dom_count - 1, step):
        some = FAR_FIRST[start : start + step]
        for s in some:
            resp_s[s] = answer(s, req_r[s])
        for s in some:
            send(resp_s, resp_r, resp_send, resp_recv, s, behind[s])

    loads[6].wait()
    wait_all(resp_r, resp_recv)
    found = [jnp.zeros((8, LANES), jnp.float32)] * (faces // LANES)
    for s in range(dom_count):
        values = resp_r[s]
        values = jnp.concatenate([values, values], axis=0)
        for c in range(faces // LANES):
            part = slice(c * LANES, (c + 1) * LANES)
            found[c] = jnp.where(
                far8[:, part] == s, take_lanes(values, pick[:, part]), found[c]
            )
    face_psi = jnp.concatenate(found, axis=1)
    coarse = face_psi.astype(jnp.bfloat16).astype(jnp.float32)
    fine = face_psi - coarse
    sums = jnp.zeros((2 * dom_count, SENS), jnp.float32)
    for v in range(NVAR):
        row = v if v < 3 else v + 1
        weights = jnp.concatenate(
            [
                jnp.where(feeds, coarse[row : row + 1], 0.0),
                jnp.where(feeds, fine[row : row + 1], 0.0),
            ],
            axis=0,
        ).astype(jnp.bfloat16)
        sums = sums + jnp.dot(
            weights,
            jac_v[:, v * SENS : (v + 1) * SENS],
            preferred_element_type=jnp.float32,
        )
    sums = sums[:dom_count] + sums[dom_count:]
    for s in range(1, dom_count):
        part_s[s] = sums[s : s + 1]
    part_r[0] = sums[0:1]
    for s in FAR_FIRST:
        send(part_s, part_r, part_send, part_recv, s, ahead[s])
    wait_all(part_r, part_recv)
    sens_v[...] = jnp.sum(part_r[...], axis=0)
    box_copy = pltpu.make_async_copy(sens_v, box_o, out_sem.at[1])
    box_copy.start()
    wait_all(req_s, req_send)
    wait_all(resp_s, resp_send)
    wait_all(part_s, part_send)
    adj_copy.wait()
    box_copy.wait()


def solution(mesh):
    groups = mesh.shape["group"]

    def shards(adjoint, gradient, precond, band, face_jac, face_cell, face_box):
        cells = adjoint.shape[1]
        faces = face_jac.shape[0]
        dom_count = X * Y
        ext = cells + LANES
        f32 = jnp.float32
        vmem = pltpu.VMEM
        dma = pltpu.SemaphoreType.DMA
        return pl.pallas_call(
            functools.partial(kernel, groups),
            out_shape=(
                jax.ShapeDtypeStruct((NVAR, cells), f32),
                jax.ShapeDtypeStruct((1, SENS), f32),
            ),
            in_specs=[pl.BlockSpec(memory_space=pl.ANY)] * 7,
            out_specs=[pl.BlockSpec(memory_space=pl.ANY)] * 2,
            scratch_shapes=[
                vmem((NVAR, cells), f32),
                vmem((NVAR, cells), f32),
                vmem((NVAR, cells), f32),
                vmem((BAND, NVAR, NVAR, cells), jnp.bfloat16),
                vmem((faces, NVAR * SENS), jnp.bfloat16),
                vmem((1, faces), jnp.int32),
                vmem((1, faces), jnp.int32),
                vmem((BAND * NVAR, NVAR, ext), f32),
                vmem((BAND, NVAR, ext), f32),
                vmem((8, cells), f32),
                vmem((NVAR, cells), f32),
                vmem((3, NVAR, LANES), f32),
                vmem((3, NVAR, LANES), f32),
                vmem((3, NVAR, LANES), f32),
                vmem((dom_count, 1, LANES), jnp.int32),
                vmem((dom_count, 1, LANES), jnp.int32),
                vmem((dom_count, 4, LANES), f32),
                vmem((dom_count, 4, LANES), f32),
                vmem((dom_count, 1, SENS), f32),
                vmem((dom_count, 1, SENS), f32),
                vmem((1, SENS), f32),
                dma((7,)),
                dma((2,)),
                dma((2,)),
                dma,
                dma,
                dma,
                dma,
                dma,
                dma,
                dma((2,)),
            ],
            compiler_params=pltpu.CompilerParams(
                collective_id=0, has_side_effects=True
            ),
        )(
            adjoint,
            gradient,
            precond,
            band,
            face_jac,
            face_cell.reshape(1, faces),
            face_box.reshape(1, faces),
        )

    return jax.shard_map(
        shards,
        mesh=mesh,
        in_specs=(
            P(None, ("group", "dom")),
            P(None, ("group", "dom")),
            P(None, ("group", "dom")),
            P(None, None, None, ("group", "dom")),
            P(("group", "dom"), None),
            P(("group", "dom")),
            P(("group", "dom"), None),
        ),
        out_specs=(P(None, ("group", "dom")), P(("group", "dom"), None)),
        check_vma=False,
    )
```

time: 248 us -> 34.7 us (0.14)
  the two profiles are of different devices: /device:TPU:256 before, /device:TPU:8 now
where the time goes in v1:
time: 34.7 us; the launch traced here: 34.4 us
  Pallas kernels  31.8 us (92%)
  local copies, waits for them, and re-layouts  1.89 us (5%)
  between operations  0.65 us (2%)
    pallas_call x1, Pallas kernels, shards(): pl.pallas_call(functools.partial(kernel, groups), out_shape=(jax.ShapeDty...  31.8 us
    unnamed x4, local copies, waits for them, and re-layouts  1.89 us

profile of v1, /device:TPU:8, one launch (start us, length us, event | category | flops | bytes accessed | tf_op | source)
XLA Modules:
  0.0 34.4 jit_solution(5784881903109449916)
XLA Ops:
  0.6 31.8 %shard_map.86 = (f32[6,1024]{1,0:T(8,128)}, f32[1,128]{1,0:T(1,128)}) custom-call(f32[6,1024]{1,0:T(8,128)} %adj_h.1, f32[6,1024]{1,0:T(8,128)} %grad_h.1, f32[6,1024]{1,0:T(8,128)} %pre_h.1, bf16[5,6,6,1024]{3,2,1,0:T(8,128)(2,1)} %band_h.1, bf16[512,768]{1,0:T(8,128)(2,1)} %jac_h.1, s32[1,512]{1,0:T(1,128)} %bitcast.2, s32[1,512]{1,0:T(1,128)} %bitcast.3), custom_call_target="tpu_custom_call" | custom-call | tf_op jit(solution)/shard_map/pallas_call | solution.py:328
  32.5 0.0 copy-start
  32.5 1.4 %copy.11 = f32[6,1024]{1,0:T(8,128)} copy(f32[6,1024]{1,0:T(8,128)} %get-tuple-element.4) | data formatting | bytes 49152
  33.8 0.0 copy-done
  33.9 0.5 %copy.12 = f32[1,128]{1,0:T(1,128)} copy(f32[1,128]{1,0:T(1,128)S(1)} %copy-done) | data formatting | bytes 1024
Async XLA Ops:
  32.5 1.4 %copy-start = (f32[1,128]{1,0:T(1,128)S(1)}, f32[1,128]{1,0:T(1,128)}, u32[]{:S(2)}) copy-start(f32[1,128]{1,0:T(1,128)} %get-tuple-element.5) | copy-start | bytes 1540

commit v2 on v1

--- a/solution.py
+++ b/solution.py
@@ -47,7 +47,6 @@
     bandf,
     shf,
     psi8,
-    out_v,
     halo_s,
     halo_l,
     halo_r,
@@ -57,7 +56,6 @@
     resp_r,
     part_s,
     part_r,
-    sens_v,
     in_sem,
     halo_send,
     halo_recv,
@@ -67,7 +65,6 @@
     resp_recv,
     part_send,
     part_recv,
-    out_sem,
 ):
     cells = adj_h.shape[1]
     faces = jac_h.shape[0]
@@ -90,14 +87,6 @@
     after_id = (after // dom_count, after % dom_count)
     before_id = (before // dom_count, before % dom_count)
 
-    barrier = pltpu.get_barrier_semaphore()
-    for target in (before_id, after_id):
-        pl.semaphore_signal(barrier, inc=1, device_id=target, device_id_type=MESH)
-    for s in FAR_FIRST:
-        pl.semaphore_signal(
-            barrier, inc=1, device_id=(g, ahead[s]), device_id_type=MESH
-        )
-
     loads = [
         pltpu.make_async_copy(src, dst, in_sem.at[i])
         for i, (src, dst) in enumerate(
@@ -114,6 +103,22 @@
     ]
     for load in loads:
         load.start()
+
+    barrier = pltpu.get_barrier_semaphore()
+    first, last = place == 0, place == total - 1
+
+    @pl.when(jnp.logical_not(first))
+    def _():
+        pl.semaphore_signal(barrier, inc=1, device_id=before_id, device_id_type=MESH)
+
+    @pl.when(jnp.logical_not(last))
+    def _():
+        pl.semaphore_signal(barrier, inc=1, device_id=after_id, device_id_type=MESH)
+
+    for s in FAR_FIRST:
+        pl.semaphore_signal(
+            barrier, inc=1, device_id=(g, ahead[s]), device_id_type=MESH
+        )
 
     loads[0].wait()
     cell = cell_v[...]
@@ -150,8 +155,9 @@
         u = t % half
         ends = pltpu.roll(ends, 8 * u + 4, 1)
         packed[t // half] = jnp.where(lane // 8 == u, ends, packed[t // half])
-    halo_s[0] = packed[0]
-    halo_s[1] = packed[1]
+    rest = jnp.zeros((8 - NVAR, LANES), jnp.float32)
+    halo_s[0] = jnp.concatenate([packed[0], rest], axis=0)
+    halo_s[1] = jnp.concatenate([packed[1], rest], axis=0)
     for load in loads[2:5]:
         load.wait()
     adj, grad, pre = adj_v[...], grad_v[...], pre_v[...]
@@ -159,14 +165,24 @@
         jnp.where(head, v[:, :LANES], v[:, cells - LANES :]) for v in (adj, grad, pre)
     ]
     near = (lane < 16) | (lane >= 112)
-    halo_s[2] = jnp.where(
+    packed = jnp.where(
         near,
         ends[0],
         jnp.where(head, pltpu.roll(ends[1], 32, 1), pltpu.roll(ends[2], 80, 1)),
     )
+    halo_s[2] = jnp.concatenate([packed, rest], axis=0)
     psi8[NVAR:, :] = jnp.zeros((8 - NVAR, cells), jnp.float32)
 
-    pl.semaphore_wait(barrier, dom_count + 1)
+    ends_of_all = first.astype(jnp.int32) + last.astype(jnp.int32)
+    pl.semaphore_wait(barrier, dom_count + 1 - ends_of_all)
+
+    @pl.when(first)
+    def _():
+        halo_l[...] = jnp.zeros_like(halo_l)
+
+    @pl.when(last)
+    def _():
+        halo_r[...] = jnp.zeros_like(halo_r)
 
     halo_copies = []
     for i, (target, landing) in enumerate(((after_id, halo_l), (before_id, halo_r))):
@@ -180,8 +196,8 @@
                 device_id_type=MESH,
             )
         )
-    for copy in halo_copies:
-        copy.start()
+    pl.when(jnp.logical_not(last))(halo_copies[0].start)
+    pl.when(jnp.logical_not(first))(halo_copies[1].start)
 
     def send(source, landing, send_sem, recv_sem, s, target):
         pltpu.make_async_remote_copy(
@@ -210,11 +226,10 @@
     box_far = ((box // X - y + Y) % Y) * X + (box % X - x + X) % X
     feeds = slots == box_far
 
-    for copy in halo_copies:
-        copy.wait()
-    first, last = place == 0, place == total - 1
-    left = jnp.where(first, 0.0, halo_l[...])
-    right = jnp.where(last, 0.0, halo_r[...])
+    pl.when(jnp.logical_not(first))(halo_copies[0].wait_recv)
+    pl.when(jnp.logical_not(last))(halo_copies[1].wait_recv)
+    left = halo_l[:, :NVAR, :]
+    right = halo_r[:, :NVAR, :]
     from_left = lane % 8 < 4
     for h in range(2):
         both = jnp.where(from_left, left[h], right[h])
@@ -240,33 +255,41 @@
             total_sum = term if total_sum is None else total_sum + term
         psi = psi[:, :width] + pre[:, :width] * (grad[:, :width] - total_sum)
     psi8[:NVAR, :] = psi
-    out_v[...] = psi
-    adj_copy = pltpu.make_async_copy(out_v, adj_o, out_sem.at[0])
-    adj_copy.start()
+    adj_o[...] = psi
 
     chunks = [psi8[:, c * LANES : (c + 1) * LANES] for c in range(blocks)]
     low8 = lax.broadcasted_iota(jnp.int32, (8, LANES), 1) < CAP
 
-    def answer(s, wish):
-        turned = pltpu.roll(wish, CAP, 1)
-        low1 = low8[:1]
-        chunk = jnp.broadcast_to(jnp.where(low1, wish, turned), (8, LANES))
-        place_in = jnp.broadcast_to(jnp.where(low1, turned, wish), (8, LANES))
+    low1 = low8[:1]
+
+    def answers(wish, other):
+        chunk = jnp.where(low1, wish, pltpu.roll(other, CAP, 1))
+        place_in = jnp.where(low1, pltpu.roll(wish, CAP, 1), other)
+        chunk = jnp.broadcast_to(chunk, (8, LANES))
+        place_in = jnp.broadcast_to(place_in, (8, LANES))
         found = take_lanes(chunks[0], place_in)
         for c in range(1, blocks):
             found = jnp.where(chunk == c, take_lanes(chunks[c], place_in), found)
-        both = jnp.where(low8, found, pltpu.roll(found, 5, 0))
-        return both[:4]
-
-    resp_r[0] = answer(0, req_s[0])
+        turned = pltpu.roll(found, 5, 0)
+        return (
+            jnp.where(low8, found, pltpu.roll(turned, CAP, 1))[:4],
+            jnp.where(low8, pltpu.roll(found, CAP, 1), turned)[:4],
+        )
+
     wait_all(req_r, req_recv)
-    step = 4
-    for start in range(0, dom_count - 1, step):
-        some = FAR_FIRST[start : start + step]
+    order = FAR_FIRST + [0]
+    step = 8
+    for start in range(0, dom_count, step):
+        some = order[start : start + step]
+        for s, t in zip(some[::2], some[1::2]):
+            resp_s[s], own = answers(req_r[s], req_r[t] if t else req_s[0])
+            if t:
+                resp_s[t] = own
+            else:
+                resp_r[0] = own
         for s in some:
-            resp_s[s] = answer(s, req_r[s])
-        for s in some:
-            send(resp_s, resp_r, resp_send, resp_recv, s, behind[s])
+            if s:
+                send(resp_s, resp_r, resp_send, resp_recv, s, behind[s])
 
     loads[6].wait()
     wait_all(resp_r, resp_recv)
@@ -304,14 +327,12 @@
     for s in FAR_FIRST:
         send(part_s, part_r, part_send, part_recv, s, ahead[s])
     wait_all(part_r, part_recv)
-    sens_v[...] = jnp.sum(part_r[...], axis=0)
-    box_copy = pltpu.make_async_copy(sens_v, box_o, out_sem.at[1])
-    box_copy.start()
+    box_o[...] = jnp.sum(part_r[...], axis=0)
     wait_all(req_s, req_send)
     wait_all(resp_s, resp_send)
     wait_all(part_s, part_send)
-    adj_copy.wait()
-    box_copy.wait()
+    pl.when(jnp.logical_not(last))(halo_copies[0].wait_send)
+    pl.when(jnp.logical_not(first))(halo_copies[1].wait_send)
 
 
 def solution(mesh):
@@ -328,11 +349,11 @@
         return pl.pallas_call(
             functools.partial(kernel, groups),
             out_shape=(
-                jax.ShapeDtypeStruct((NVAR, cells), f32),
-                jax.ShapeDtypeStruct((1, SENS), f32),
+                vmem((NVAR, cells), f32),
+                vmem((1, SENS), f32),
             ),
             in_specs=[pl.BlockSpec(memory_space=pl.ANY)] * 7,
-            out_specs=[pl.BlockSpec(memory_space=pl.ANY)] * 2,
+            out_specs=[pl.BlockSpec(memory_space=pltpu.VMEM)] * 2,
             scratch_shapes=[
                 vmem((NVAR, cells), f32),
                 vmem((NVAR, cells), f32),
@@ -344,17 +365,15 @@
                 vmem((BAND * NVAR, NVAR, ext), f32),
                 vmem((BAND, NVAR, ext), f32),
                 vmem((8, cells), f32),
-                vmem((NVAR, cells), f32),
-                vmem((3, NVAR, LANES), f32),
-                vmem((3, NVAR, LANES), f32),
-                vmem((3, NVAR, LANES), f32),
+                vmem((3, 8, LANES), f32),
+                vmem((3, 8, LANES), f32),
+                vmem((3, 8, LANES), f32),
                 vmem((dom_count, 1, LANES), jnp.int32),
                 vmem((dom_count, 1, LANES), jnp.int32),
                 vmem((dom_count, 4, LANES), f32),
                 vmem((dom_count, 4, LANES), f32),
                 vmem((dom_count, 1, SENS), f32),
                 vmem((dom_count, 1, SENS), f32),
-                vmem((1, SENS), f32),
                 dma((7,)),
                 dma((2,)),
                 dma((2,)),
@@ -364,7 +383,6 @@
                 dma,
                 dma,
                 dma,
-                dma((2,)),
             ],
             compiler_params=pltpu.CompilerParams(
                 collective_id=0, has_side_effects=True

time: 34.7 us -> 29.5 us (0.85)
  the two profiles are of different devices: /device:TPU:8 before, /device:TPU:2 now
where the time goes in v2:
time: 29.5 us; the launch traced here: 29.4 us
  Pallas kernels  27.6 us (94%)
  local copies, waits for them, and re-layouts  1.13 us (4%)
  between operations  0.64 us (2%)
    pallas_call x1, Pallas kernels, shards(): pl.pallas_call(functools.partial(kernel, groups), out_shape=(vmem((NVAR,...  27.6 us
    unnamed x2, local copies, waits for them, and re-layouts  1.13 us

profile of v2, /device:TPU:2, one launch (start us, length us, event | category | flops | bytes accessed | tf_op | source)
XLA Modules:
  0.0 29.4 jit_solution(17576032465137142357)
XLA Ops:
  0.6 27.6 %shard_map.86 = (f32[6,1024]{1,0:T(8,128)S(1)}, f32[1,128]{1,0:T(1,128)S(1)}) custom-call(f32[6,1024]{1,0:T(8,128)} %adj_h.1, f32[6,1024]{1,0:T(8,128)} %grad_h.1, f32[6,1024]{1,0:T(8,128)} %pre_h.1, bf16[5,6,6,1024]{3,2,1,0:T(8,128)(2,1)} %band_h.1, bf16[512,768]{1,0:T(8,128)(2,1)} %jac_h.1, s32[1,512]{1,0:T(1,128)} %bitcast.2, s32[1,512]{1,0:T(1,128)} %bitcast.3), custom_call_target="tpu_custom_call" | custom-call | tf_op jit(solution)/shard_map/pallas_call | solution.py:349
  28.3 0.6 %copy.11 = f32[6,1024]{1,0:T(8,128)} copy(f32[6,1024]{1,0:T(8,128)S(1)} %get-tuple-element.2) | data formatting | bytes 49152
  28.9 0.5 %copy.12 = f32[1,128]{1,0:T(1,128)} copy(f32[1,128]{1,0:T(1,128)S(1)} %get-tuple-element.3) | data formatting | bytes 1024

commit v3 on v2

v3 whole, which is shorter than its diff:
```python
import functools

import jax
import jax.numpy as jnp
from jax import lax
from jax.experimental import pallas as pl
from jax.experimental.pallas import tpu as pltpu
from jax.sharding import PartitionSpec as P

NVAR = 6
SENS = 128
BAND = 5
SWEEPS = 3
CAP = 64
LANES = 128
X, Y = 4, 8
MESH = pl.DeviceIdType.MESH

FAR_FIRST = sorted(
    range(1, X * Y),
    key=lambda s: -(min(s % X, X - s % X) + min(s // X, Y - s // X)),
)
NEAR, FAR = (6, 7, 1, 2), (3, 4, 5)
SLOT = {dy: i for i, dy in enumerate(NEAR + FAR)}


def take_lanes(values, index):
    return jnp.take_along_axis(values, index, axis=1, mode="promise_in_bounds")


def sweep(psi, grad, pre, band_ref, shifted_ref, width):
    for _ in range(SWEEPS):
        for k in range(BAND):
            shifted_ref[k, :, :width] = (
                psi if k == 2 else pltpu.roll(psi, (2 - k) % width, 1)
            )
        sums = []
        for k in range(BAND):
            part = None
            for b in range(NVAR):
                column = jnp.broadcast_to(
                    shifted_ref[k, b : b + 1, :width], (NVAR, width)
                )
                term = band_ref[k * NVAR + b] * column
                part = term if part is None else part + term
            sums.append(part)
        total = (sums[0] + sums[1]) + (sums[2] + sums[3]) + sums[4]
        psi = psi + pre * (grad - total)
    return psi


def kernel(
    groups,
    adj_h,
    grad_h,
    pre_h,
    band_h,
    jac_h,
    cell_h,
    box_h,
    out_o,
    adj_v,
    grad_v,
    pre_v,
    band_v,
    jac_v,
    cell_v,
    box_v,
    bandf,
    band_edge,
    shf,
    halo_s,
    halo_l,
    halo_r,
    psi_s,
    psi_r,
    req_s,
    req_r,
    req_own,
    resp_s,
    resp_r,
    resp_own,
    part_s,
    part_r,
    in_sem,
    halo_send,
    halo_recv,
    known,
    psi_send,
    psi_recv,
    req_send,
    req_recv,
    resp_send,
    resp_recv,
    part_send,
    part_recv,
):
    cells = adj_h.shape[1]
    faces = jac_h.shape[0]
    dom_count = X * Y
    blocks = cells // LANES
    tiles = blocks * NVAR // 8
    g = lax.axis_index("group")
    d = lax.axis_index("dom")
    y, x = d // X, d % X
    rows = [((y + dy) % Y) * X for dy in range(Y)]
    columns = [(x + dx) % X for dx in range(X)]
    ahead = [rows[s // X] + columns[s % X] for s in range(dom_count)]
    total = groups * dom_count
    place = g * dom_count + d
    after = (place + 1) % total
    before = (place + total - 1) % total
    after_id = (after // dom_count, after % dom_count)
    before_id = (before // dom_count, before % dom_count)
    first, last = place == 0, place == total - 1

    loads = [
        pltpu.make_async_copy(src, dst, in_sem.at[i])
        for i, (src, dst) in enumerate(
            (
                (band_h, band_v),
                (adj_h, adj_v),
                (grad_h, grad_v),
                (pre_h, pre_v),
                (cell_h, cell_v),
                (box_h, box_v),
                (jac_h, jac_v),
            )
        )
    ]
    for load in loads:
        load.start()

    barrier = pltpu.get_barrier_semaphore()

    def greet(target):
        pl.semaphore_signal(barrier, inc=1, device_id=target, device_id_type=MESH)

    near = [X * dy for dy in NEAR] + list(range(1, X))
    for s in near:
        greet((g, ahead[s]))
    pl.when(jnp.logical_not(first))(lambda: greet(before_id))
    pl.when(jnp.logical_not(last))(lambda: greet(after_id))

    lane = lax.broadcasted_iota(jnp.int32, (NVAR, LANES), 1)
    head = lane < CAP
    half = BAND * NVAR // 2
    packed = [jnp.zeros((NVAR, LANES), jnp.float32)] * 2
    loads[0].wait()
    for t in range(BAND * NVAR):
        tile = band_v[t // NVAR, t % NVAR].astype(jnp.float32)
        bandf[t] = tile
        start, end = tile[:, :LANES], tile[:, cells - LANES :]
        band_edge[t, :, :LANES] = end
        band_edge[t, :, 2 * LANES :] = start
        u = t % half
        ends = pltpu.roll(jnp.where(head, start, end), 8 * u + 4, 1)
        packed[t // half] = jnp.where(lane // 8 == u, ends, packed[t // half])
    rest = jnp.zeros((8 - NVAR, LANES), jnp.float32)
    halo_s[0] = jnp.concatenate([packed[0], rest], axis=0)
    halo_s[1] = jnp.concatenate([packed[1], rest], axis=0)
    for load in loads[1:4]:
        load.wait()
    adj, grad, pre = adj_v[...], grad_v[...], pre_v[...]
    ends = [
        jnp.where(head, v[:, :LANES], v[:, cells - LANES :]) for v in (adj, grad, pre)
    ]
    packed = jnp.where(
        (lane < 16) | (lane >= 112),
        ends[0],
        jnp.where(head, pltpu.roll(ends[1], 32, 1), pltpu.roll(ends[2], 80, 1)),
    )
    halo_s[2] = jnp.concatenate([packed, rest], axis=0)

    @pl.when(first)
    def _():
        halo_l[...] = jnp.zeros_like(halo_l)

    @pl.when(last)
    def _():
        halo_r[...] = jnp.zeros_like(halo_r)

    missing = first.astype(jnp.int32) + last.astype(jnp.int32)
    pl.semaphore_wait(barrier, len(near) + 2 - missing)

    halo_copies = []
    for i, (target, landing) in enumerate(((after_id, halo_l), (before_id, halo_r))):
        halo_copies.append(
            pltpu.make_async_remote_copy(
                src_ref=halo_s,
                dst_ref=landing,
                send_sem=halo_send.at[i],
                recv_sem=halo_recv.at[i],
                device_id=target,
                device_id_type=MESH,
            )
        )
    pl.when(jnp.logical_not(last))(halo_copies[0].start)
    pl.when(jnp.logical_not(first))(halo_copies[1].start)

    for dy in (2, 6):
        pl.semaphore_signal(
            known, inc=1, device_id=(g, ahead[X * dy]), device_id_type=MESH
        )

    loads[4].wait()
    cell = cell_v[...]
    owner, local = cell // cells, cell % cells
    far = ((owner // X - y + Y) % Y) * X + (owner % X - x + X) % X
    slots = lax.broadcasted_iota(jnp.int32, (dom_count, faces), 0)
    reads = jnp.where(slots == far, 1.0, 0.0)
    earlier = lax.broadcasted_iota(jnp.int32, (faces, faces), 0)
    later = lax.broadcasted_iota(jnp.int32, (faces, faces), 1)
    upper = jnp.where(earlier < later, 1.0, 0.0).astype(jnp.bfloat16)
    reads_b = reads.astype(jnp.bfloat16)
    counts = jnp.dot(reads_b, upper, preferred_element_type=jnp.float32)
    rank = jnp.sum(reads * counts, axis=0, keepdims=True).astype(jnp.int32)
    lines = lax.broadcasted_iota(jnp.int32, (2 * CAP, faces), 0)
    wanted = jnp.where(
        lines < CAP, (local // LANES).astype(jnp.float32), (local % LANES).astype(jnp.float32)
    )
    wanted = jnp.where(lines % CAP == rank, wanted, 0.0).astype(jnp.bfloat16)
    requests = lax.dot_general(
        reads_b, wanted, (((1,), (1,)), ((), ())), preferred_element_type=jnp.float32
    ).astype(jnp.int32)
    req_own[...] = requests[:X]
    for dy in range(1, Y):
        req_s[SLOT[dy]] = requests[X * dy : X * dy + X]

    def send(source, landing, send_sem, recv_sem, target):
        pltpu.make_async_remote_copy(
            src_ref=source,
            dst_ref=landing,
            send_sem=send_sem,
            recv_sem=recv_sem,
            device_id=(g, target),
            device_id_type=MESH,
        ).start()

    def wait_all(ref, start, count, sem):
        some = ref.at[pl.ds(start, count)]
        pltpu.make_async_copy(some, some, sem).wait()

    pl.semaphore_wait(known, 2)
    for dy in (4, 3, 5, 2, 6, 1, 7):
        i = SLOT[dy]
        send(req_s.at[i], req_r.at[i], req_send, req_recv, ahead[X * dy])

    inner = sweep(adj, grad, pre, bandf, shf, cells)

    pick = jnp.broadcast_to(rank, (8, faces)) + jnp.where(
        lax.broadcasted_iota(jnp.int32, (8, faces), 0) < 3, 0, CAP
    )
    far8 = jnp.broadcast_to(far, (8, faces))
    loads[5].wait()
    box = box_v[...]
    box_far = ((box // X - y + Y) % Y) * X + (box % X - x + X) % X
    feeds = slots == box_far

    pl.when(jnp.logical_not(first))(halo_copies[0].wait_recv)
    pl.when(jnp.logical_not(last))(halo_copies[1].wait_recv)
    left = halo_l[:, :NVAR, :]
    right = halo_r[:, :NVAR, :]
    from_left = lane % 8 < 4
    for h in range(2):
        both = jnp.where(from_left, left[h], right[h])
        for u in range(half):
            band_edge[h * half + u, :, LANES : 2 * LANES] = pltpu.roll(
                both, LANES - (8 * u + 4), 1
            )

    def edge(v, turn):
        between = jnp.where(head, right[2], left[2])
        if turn:
            between = jnp.where(
                head, pltpu.roll(right[2], turn, 1), pltpu.roll(left[2], turn, 1)
            )
        return jnp.concatenate(
            [v[:, cells - LANES :], between, v[:, :LANES]], axis=1
        )

    outer = sweep(
        edge(adj, 0), edge(grad, 96), edge(pre, 48), band_edge, shf, 3 * LANES
    )
    psi = [inner[:, c * LANES : (c + 1) * LANES] for c in range(blocks)]
    psi[0] = jnp.where(head, outer[:, 2 * LANES :], psi[0])
    psi[-1] = jnp.where(head, psi[-1], outer[:, :LANES])
    spare = jnp.concatenate(psi[tiles:], axis=0)
    for c in range(tiles):
        part = slice(c * LANES, (c + 1) * LANES)
        psi_s[:, part] = jnp.concatenate([psi[c], spare[2 * c : 2 * c + 2]], axis=0)
    for dx in (2, 1, 3):
        i = X - dx
        send(psi_s, psi_r.at[i], psi_send, psi_recv, ahead[dx])
    for c in range(blocks):
        out_o[:NVAR, c * LANES : (c + 1) * LANES] = psi[c]
    out_o[NVAR:, :] = jnp.zeros((8 - NVAR, cells), jnp.float32)

    low8 = lax.broadcasted_iota(jnp.int32, (8, LANES), 1) < CAP
    low1 = low8[:1]

    def row_values(ref):
        parts = [ref[:, c * LANES : (c + 1) * LANES] for c in range(tiles)]
        size = 8 - NVAR
        for start in range(0, tiles, NVAR // size):
            some = [p[NVAR:] for p in parts[start : start + NVAR // size]]
            parts.append(jnp.concatenate(some + some[:1], axis=0))
        return parts

    def answers(values, wish, other):
        chunk = jnp.where(low1, wish, pltpu.roll(other, CAP, 1))
        place_in = jnp.where(low1, pltpu.roll(wish, CAP, 1), other)
        chunk = jnp.broadcast_to(chunk, (8, LANES))
        place_in = jnp.broadcast_to(place_in, (8, LANES))
        found = take_lanes(values[0], place_in)
        for c in range(1, blocks):
            found = jnp.where(chunk == c, take_lanes(values[c], place_in), found)
        turned = pltpu.roll(found, 5, 0)
        return (
            jnp.where(low8, found, pltpu.roll(turned, CAP, 1))[:3],
            jnp.where(low8, pltpu.roll(found, CAP, 1), turned)[:3],
        )

    pairs = ((4, 3), (5, 2), (6, 1), (7, 0))

    def answer(values, dx, pair):
        a, b = pair
        wish = req_r[SLOT[a], dx : dx + 1]
        other = req_r[SLOT[b], dx : dx + 1] if b else req_own[dx : dx + 1]
        one, two = answers(values, wish, other)
        resp_s[SLOT[a], 3 * dx : 3 * dx + 3] = one
        if b:
            resp_s[SLOT[b], 3 * dx : 3 * dx + 3] = two
        else:
            resp_own[3 * dx : 3 * dx + 3] = two

    wait_all(req_r, 0, Y - 1, req_recv)
    own_values = row_values(psi_s)
    for pair in pairs:
        answer(own_values, 0, pair)
    wait_all(psi_r, 1, X - 1, psi_recv)
    values = [row_values(psi_r.at[dx]) for dx in range(1, X)]
    for pair in pairs:
        for dx in range(1, X):
            answer(values[dx - 1], dx, pair)
        for dy in pair:
            if dy:
                i = SLOT[dy]
                send(
                    resp_s.at[i],
                    resp_r.at[i],
                    resp_send,
                    resp_recv.at[0 if dy in NEAR else 1],
                    ahead[X * (Y - dy)],
                )

    found = [jnp.zeros((8, LANES), jnp.float32)] * (faces // LANES)

    def look(dy, ref):
        for dx in range(X):
            got = ref[3 * dx : 3 * dx + 3]
            got = jnp.concatenate([got, got, got[:2]], axis=0)
            for c in range(faces // LANES):
                part = slice(c * LANES, (c + 1) * LANES)
                found[c] = jnp.where(
                    far8[:, part] == dy * X + dx, take_lanes(got, pick[:, part]), found[c]
                )

    look(0, resp_own)
    wait_all(resp_r, 0, len(NEAR), resp_recv.at[0])
    for dy in NEAR:
        look(dy, resp_r.at[SLOT[dy]])
    loads[6].wait()
    wait_all(resp_r, len(NEAR), len(FAR), resp_recv.at[1])
    for dy in FAR:
        look(dy, resp_r.at[SLOT[dy]])
    face_psi = jnp.concatenate(found, axis=1)
    coarse = face_psi.astype(jnp.bfloat16).astype(jnp.float32)
    fine = face_psi - coarse
    sums = jnp.zeros((2 * dom_count, SENS), jnp.float32)
    for v in range(NVAR):
        weights = jnp.concatenate(
            [
                jnp.where(feeds, coarse[v : v + 1], 0.0),
                jnp.where(feeds, fine[v : v + 1], 0.0),
            ],
            axis=0,
        ).astype(jnp.bfloat16)
        sums = sums + jnp.dot(
            weights,
            jac_v[:, v * SENS : (v + 1) * SENS],
            preferred_element_type=jnp.float32,
        )
    sums = sums[:dom_count] + sums[dom_count:]
    for s in range(1, dom_count):
        part_s[s] = sums[s : s + 1]
    part_r[0] = sums[0:1]
    for s in FAR_FIRST:
        send(part_s.at[s], part_r.at[s], part_send, part_recv, ahead[s])
    wait_all(part_r, 1, dom_count - 1, part_recv)
    out_o[NVAR : NVAR + 1, :SENS] = jnp.sum(part_r[...], axis=0)
    pl.when(jnp.logical_not(last))(halo_copies[0].wait_send)
    pl.when(jnp.logical_not(first))(halo_copies[1].wait_send)
    wait_all(req_s, 0, Y - 1, req_send)
    wait_all(psi_r, 1, X - 1, psi_send)
    wait_all(resp_s, 0, Y - 1, resp_send)
    wait_all(part_s, 1, dom_count - 1, part_send)


def solution(mesh):
    groups = mesh.shape["group"]

    def shards(adjoint, gradient, precond, band, face_jac, face_cell, face_box):
        cells = adjoint.shape[1]
        faces = face_jac.shape[0]
        dom_count = X * Y
        packed = cells * NVAR // 8
        f32 = jnp.float32
        vmem = pltpu.VMEM
        dma = pltpu.SemaphoreType.DMA
        out = pl.pallas_call(
            functools.partial(kernel, groups),
            out_shape=vmem((8, cells), f32),
            in_specs=[pl.BlockSpec(memory_space=pl.ANY)] * 7,
            out_specs=pl.BlockSpec(memory_space=pltpu.VMEM),
            scratch_shapes=[
                vmem((NVAR, cells), f32),
                vmem((NVAR, cells), f32),
                vmem((NVAR, cells), f32),
                vmem((BAND, NVAR, NVAR, cells), jnp.bfloat16),
                vmem((faces, NVAR * SENS), jnp.bfloat16),
                vmem((1, faces), jnp.int32),
                vmem((1, faces), jnp.int32),
                vmem((BAND * NVAR, NVAR, cells), f32),
                vmem((BAND * NVAR, NVAR, 3 * LANES), f32),
                vmem((BAND, NVAR, cells), f32),
                vmem((3, 8, LANES), f32),
                vmem((3, 8, LANES), f32),
                vmem((3, 8, LANES), f32),
                vmem((8, packed), f32),
                vmem((X, 8, packed), f32),
                vmem((Y - 1, X, LANES), jnp.int32),
                vmem((Y - 1, X, LANES), jnp.int32),
                vmem((X, LANES), jnp.int32),
                vmem((Y - 1, 3 * X, LANES), f32),
                vmem((Y - 1, 3 * X, LANES), f32),
                vmem((3 * X, LANES), f32),
                vmem((dom_count, 1, LANES), f32),
                vmem((dom_count, 1, LANES), f32),
                dma((7,)),
                dma((2,)),
                dma((2,)),
                pltpu.SemaphoreType.REGULAR,
                dma,
                dma,
                dma,
                dma,
                dma,
                dma((2,)),
                dma,
                dma,
            ],
            compiler_params=pltpu.CompilerParams(
                collective_id=0, has_side_effects=True
            ),
        )(
            adjoint,
            gradient,
            precond,
            band,
            face_jac,
            face_cell.reshape(1, faces),
            face_box.reshape(1, faces),
        )
        return out[:NVAR], out[NVAR : NVAR + 1, :SENS]

    return jax.shard_map(
        shards,
        mesh=mesh,
        in_specs=(
            P(None, ("group", "dom")),
            P(None, ("group", "dom")),
            P(None, ("group", "dom")),
            P(None, None, None, ("group", "dom")),
            P(("group", "dom"), None),
            P(("group", "dom")),
            P(("group", "dom"), None),
        ),
        out_specs=(P(None, ("group", "dom")), P(("group", "dom"), None)),
        check_vma=False,
    )
```

time: 29.5 us -> 27.9 us (0.946)
  the two profiles are of different devices: /device:TPU:2 before, /device:TPU:8 now
where the time goes in v3:
time: 27.9 us; the launch traced here: 27.8 us
  Pallas kernels  26 us (93%)
  local copies, waits for them, and re-layouts  1.13 us (4%)
  between operations  0.64 us (2%)
    pallas_call x1, Pallas kernels, shards(): pl.pallas_call(functools.partial(kernel, groups), out_shape=vmem((8, cell...  26 us
    unnamed x1, local copies, waits for them, and re-layouts  0.61 us

profile of v3, /device:TPU:8, one launch (start us, length us, event | category | flops | bytes accessed | tf_op | source)
XLA Modules:
  0.0 27.8 jit_solution(7132266030479214973)
XLA Ops:
  0.6 26.0 %shard_map.86 = f32[8,1024]{1,0:T(8,128)S(1)} custom-call(f32[6,1024]{1,0:T(8,128)} %adj_h.1, f32[6,1024]{1,0:T(8,128)} %grad_h.1, f32[6,1024]{1,0:T(8,128)} %pre_h.1, bf16[5,6,6,1024]{3,2,1,0:T(8,128)(2,1)} %band_h.1, bf16[512,768]{1,0:T(8,128)(2,1)} %jac_h.1, s32[1,512]{1,0:T(1,128)} %bitcast.4, s32[1,512]{1,0:T(1,128)} %bitcast.5), custom_call_target="tpu_custom_call" | custom-call | tf_op jit(solution)/shard_map/pallas_call | solution.py:421
  26.7 0.5 %slice.7 = f32[1,128]{1,0:T(1,128)} slice(f32[8,1024]{1,0:T(8,128)S(1)} %shard_map.86), slice={[6:7], [0:128]} | slice | bytes 1024 | tf_op jit(solution)/shard_map/slice | solution.py:475
  27.2 0.6 %copy.10 = f32[6,1024]{1,0:T(8,128)} copy(f32[6,1024]{1,0:T(8,128)S(1)} %bitcast.3) | data formatting | bytes 49152

commit v4 on v3

--- a/solution.py
+++ b/solution.py
@@ -12,6 +12,7 @@
 BAND = 5
 SWEEPS = 3
 CAP = 64
+HALO = 2 * SWEEPS
 LANES = 128
 X, Y = 4, 8
 MESH = pl.DeviceIdType.MESH
@@ -80,18 +81,21 @@
     resp_s,
     resp_r,
     resp_own,
+    ends_s,
+    ends_r,
     part_s,
     part_r,
     in_sem,
     halo_send,
     halo_recv,
-    known,
     psi_send,
     psi_recv,
     req_send,
     req_recv,
     resp_send,
     resp_recv,
+    ends_send,
+    ends_recv,
     part_send,
     part_recv,
 ):
@@ -136,8 +140,8 @@
     def greet(target):
         pl.semaphore_signal(barrier, inc=1, device_id=target, device_id_type=MESH)
 
-    near = [X * dy for dy in NEAR] + list(range(1, X))
-    for s in near:
+    lines = [X * dy for dy in (4, 3, 5, 2, 6, 1, 7)] + [2, 1, 3]
+    for s in lines:
         greet((g, ahead[s]))
     pl.when(jnp.logical_not(first))(lambda: greet(before_id))
     pl.when(jnp.logical_not(last))(lambda: greet(after_id))
@@ -180,8 +184,53 @@
     def _():
         halo_r[...] = jnp.zeros_like(halo_r)
 
+    loads[4].wait()
+    cell = cell_v[...]
+    owner, local = cell // cells, cell % cells
+    far = ((owner // X - y + Y) % Y) * X + (owner % X - x + X) % X
+    slots = lax.broadcasted_iota(jnp.int32, (dom_count, faces), 0)
+    reads = jnp.where(slots == far, 1.0, 0.0)
+    earlier = lax.broadcasted_iota(jnp.int32, (faces, faces), 0)
+    later = lax.broadcasted_iota(jnp.int32, (faces, faces), 1)
+    upper = jnp.where(earlier < later, 1.0, 0.0).astype(jnp.bfloat16)
+    reads_b = reads.astype(jnp.bfloat16)
+    counts = jnp.dot(reads_b, upper, preferred_element_type=jnp.float32)
+    rank = jnp.sum(reads * counts, axis=0, keepdims=True).astype(jnp.int32)
+    entry = lax.broadcasted_iota(jnp.int32, (2 * CAP, faces), 0)
+    wanted = jnp.where(
+        entry < CAP, (local // LANES).astype(jnp.float32), (local % LANES).astype(jnp.float32)
+    )
+    wanted = jnp.where(entry % CAP == rank, wanted, 0.0).astype(jnp.bfloat16)
+    requests = lax.dot_general(
+        reads_b, wanted, (((1,), (1,)), ((), ())), preferred_element_type=jnp.float32
+    ).astype(jnp.int32)
+    req_own[...] = requests[:X]
+    for dy in range(1, Y):
+        req_s[SLOT[dy]] = requests[X * dy : X * dy + X]
+
+    def send(source, landing, send_sem, recv_sem, target):
+        pltpu.make_async_remote_copy(
+            src_ref=source,
+            dst_ref=landing,
+            send_sem=send_sem,
+            recv_sem=recv_sem,
+            device_id=(g, target),
+            device_id_type=MESH,
+        ).start()
+
+    def wait_all(ref, start, count, sem):
+        some = ref.at[pl.ds(start, count)]
+        pltpu.make_async_copy(some, some, sem).wait()
+
+    inner = sweep(adj, grad, pre, bandf, shf, cells)
+    psi = [inner[:, c * LANES : (c + 1) * LANES] for c in range(blocks)]
+    spare = jnp.concatenate(psi[tiles:], axis=0)
+    for c in range(tiles):
+        part = slice(c * LANES, (c + 1) * LANES)
+        psi_s[:, part] = jnp.concatenate([psi[c], spare[2 * c : 2 * c + 2]], axis=0)
+
     missing = first.astype(jnp.int32) + last.astype(jnp.int32)
-    pl.semaphore_wait(barrier, len(near) + 2 - missing)
+    pl.semaphore_wait(barrier, len(lines) + 2 - missing)
 
     halo_copies = []
     for i, (target, landing) in enumerate(((after_id, halo_l), (before_id, halo_r))):
@@ -198,55 +247,12 @@
     pl.when(jnp.logical_not(last))(halo_copies[0].start)
     pl.when(jnp.logical_not(first))(halo_copies[1].start)
 
-    for dy in (2, 6):
-        pl.semaphore_signal(
-            known, inc=1, device_id=(g, ahead[X * dy]), device_id_type=MESH
-        )
-
-    loads[4].wait()
-    cell = cell_v[...]
-    owner, local = cell // cells, cell % cells
-    far = ((owner // X - y + Y) % Y) * X + (owner % X - x + X) % X
-    slots = lax.broadcasted_iota(jnp.int32, (dom_count, faces), 0)
-    reads = jnp.where(slots == far, 1.0, 0.0)
-    earlier = lax.broadcasted_iota(jnp.int32, (faces, faces), 0)
-    later = lax.broadcasted_iota(jnp.int32, (faces, faces), 1)
-    upper = jnp.where(earlier < later, 1.0, 0.0).astype(jnp.bfloat16)
-    reads_b = reads.astype(jnp.bfloat16)
-    counts = jnp.dot(reads_b, upper, preferred_element_type=jnp.float32)
-    rank = jnp.sum(reads * counts, axis=0, keepdims=True).astype(jnp.int32)
-    lines = lax.broadcasted_iota(jnp.int32, (2 * CAP, faces), 0)
-    wanted = jnp.where(
-        lines < CAP, (local // LANES).astype(jnp.float32), (local % LANES).astype(jnp.float32)
-    )
-    wanted = jnp.where(lines % CAP == rank, wanted, 0.0).astype(jnp.bfloat16)
-    requests = lax.dot_general(
-        reads_b, wanted, (((1,), (1,)), ((), ())), preferred_element_type=jnp.float32
-    ).astype(jnp.int32)
-    req_own[...] = requests[:X]
-    for dy in range(1, Y):
-        req_s[SLOT[dy]] = requests[X * dy : X * dy + X]
-
-    def send(source, landing, send_sem, recv_sem, target):
-        pltpu.make_async_remote_copy(
-            src_ref=source,
-            dst_ref=landing,
-            send_sem=send_sem,
-            recv_sem=recv_sem,
-            device_id=(g, target),
-            device_id_type=MESH,
-        ).start()
-
-    def wait_all(ref, start, count, sem):
-        some = ref.at[pl.ds(start, count)]
-        pltpu.make_async_copy(some, some, sem).wait()
-
-    pl.semaphore_wait(known, 2)
+    for dx in (2, 1, 3):
+        i = X - dx
+        send(psi_s, psi_r.at[i], psi_send, psi_recv, ahead[dx])
     for dy in (4, 3, 5, 2, 6, 1, 7):
         i = SLOT[dy]
         send(req_s.at[i], req_r.at[i], req_send, req_recv, ahead[X * dy])
-
-    inner = sweep(adj, grad, pre, bandf, shf, cells)
 
     pick = jnp.broadcast_to(rank, (8, faces)) + jnp.where(
         lax.broadcasted_iota(jnp.int32, (8, faces), 0) < 3, 0, CAP
@@ -256,6 +262,10 @@
     box = box_v[...]
     box_far = ((box // X - y + Y) % Y) * X + (box % X - x + X) % X
     feeds = slots == box_far
+    at_start, at_end = local < HALO, local >= cells - HALO
+    end_place = jnp.where(at_start, local + HALO, local - (cells - HALO))
+    takes_end = lax.broadcasted_iota(jnp.int32, (16, faces), 0) == end_place
+    reads_end = at_start | at_end
 
     pl.when(jnp.logical_not(first))(halo_copies[0].wait_recv)
     pl.when(jnp.logical_not(last))(halo_copies[1].wait_recv)
@@ -282,16 +292,20 @@
     outer = sweep(
         edge(adj, 0), edge(grad, 96), edge(pre, 48), band_edge, shf, 3 * LANES
     )
-    psi = [inner[:, c * LANES : (c + 1) * LANES] for c in range(blocks)]
     psi[0] = jnp.where(head, outer[:, 2 * LANES :], psi[0])
     psi[-1] = jnp.where(head, psi[-1], outer[:, :LANES])
-    spare = jnp.concatenate(psi[tiles:], axis=0)
-    for c in range(tiles):
-        part = slice(c * LANES, (c + 1) * LANES)
-        psi_s[:, part] = jnp.concatenate([psi[c], spare[2 * c : 2 * c + 2]], axis=0)
-    for dx in (2, 1, 3):
-        i = X - dx
-        send(psi_s, psi_r.at[i], psi_send, psi_recv, ahead[dx])
+    ends = jnp.where(head, psi[0], psi[-1])
+    row = jnp.zeros((NVAR, LANES), jnp.float32)
+    which = lax.broadcasted_iota(jnp.int32, (NVAR, LANES), 0)
+    for v in range(NVAR):
+        row = jnp.where(which == v, pltpu.roll(ends, 16 * v + HALO, 1), row)
+    row = jnp.sum(jnp.where(lane // 16 == which, row, 0.0), axis=0, keepdims=True)
+    ends_s[...] = row
+    ends_r[0] = row
+    wait_all(psi_r, 1, X - 1, psi_recv)
+    for s in FAR_FIRST:
+        back = (Y - s // X) % Y * X + (X - s % X) % X
+        send(ends_s, ends_r.at[back], ends_send, ends_recv, ahead[s])
     for c in range(blocks):
         out_o[:NVAR, c * LANES : (c + 1) * LANES] = psi[c]
     out_o[NVAR:, :] = jnp.zeros((8 - NVAR, cells), jnp.float32)
@@ -335,14 +349,10 @@
             resp_own[3 * dx : 3 * dx + 3] = two
 
     wait_all(req_r, 0, Y - 1, req_recv)
-    own_values = row_values(psi_s)
+    values = [row_values(psi_s)] + [row_values(psi_r.at[dx]) for dx in range(1, X)]
     for pair in pairs:
-        answer(own_values, 0, pair)
-    wait_all(psi_r, 1, X - 1, psi_recv)
-    values = [row_values(psi_r.at[dx]) for dx in range(1, X)]
-    for pair in pairs:
-        for dx in range(1, X):
-            answer(values[dx - 1], dx, pair)
+        for dx in range(X):
+            answer(values[dx], dx, pair)
         for dy in pair:
             if dy:
                 i = SLOT[dy]
@@ -375,16 +385,26 @@
     for dy in FAR:
         look(dy, resp_r.at[SLOT[dy]])
     face_psi = jnp.concatenate(found, axis=1)
-    coarse = face_psi.astype(jnp.bfloat16).astype(jnp.float32)
-    fine = face_psi - coarse
+
+    wait_all(ends_r, 1, dom_count - 1, ends_recv)
+    ends = ends_r[...].reshape(dom_count, LANES)
+    coarse = ends.astype(jnp.bfloat16)
+    fine = (ends - coarse.astype(jnp.float32)).astype(jnp.bfloat16)
+    picked = lax.dot_general(
+        jnp.concatenate([coarse, fine], axis=0),
+        jnp.concatenate([reads_b, reads_b], axis=0),
+        (((0,), (0,)), ((), ())),
+        preferred_element_type=jnp.float32,
+    )
     sums = jnp.zeros((2 * dom_count, SENS), jnp.float32)
     for v in range(NVAR):
+        end = jnp.where(takes_end, picked[16 * v : 16 * v + 16], 0.0)
+        end = jnp.sum(end, axis=0, keepdims=True)
+        value = jnp.where(reads_end, end, face_psi[v : v + 1])
+        coarse = value.astype(jnp.bfloat16).astype(jnp.float32)
+        fine = value - coarse
         weights = jnp.concatenate(
-            [
-                jnp.where(feeds, coarse[v : v + 1], 0.0),
-                jnp.where(feeds, fine[v : v + 1], 0.0),
-            ],
-            axis=0,
+            [jnp.where(feeds, coarse, 0.0), jnp.where(feeds, fine, 0.0)], axis=0
         ).astype(jnp.bfloat16)
         sums = sums + jnp.dot(
             weights,
@@ -404,6 +424,7 @@
     wait_all(req_s, 0, Y - 1, req_send)
     wait_all(psi_r, 1, X - 1, psi_send)
     wait_all(resp_s, 0, Y - 1, resp_send)
+    wait_all(ends_r, 1, dom_count - 1, ends_send)
     wait_all(part_s, 1, dom_count - 1, part_send)
 
 
@@ -445,18 +466,21 @@
                 vmem((Y - 1, 3 * X, LANES), f32),
                 vmem((Y - 1, 3 * X, LANES), f32),
                 vmem((3 * X, LANES), f32),
+                vmem((1, LANES), f32),
+                vmem((dom_count, 1, LANES), f32),
                 vmem((dom_count, 1, LANES), f32),
                 vmem((dom_count, 1, LANES), f32),
                 dma((7,)),
                 dma((2,)),
                 dma((2,)),
-                pltpu.SemaphoreType.REGULAR,
                 dma,
                 dma,
                 dma,
                 dma,
                 dma,
                 dma((2,)),
+                dma,
+                dma,
                 dma,
                 dma,
             ],

time: 27.9 us -> 26.7 us (0.957)
  Pallas kernels: 26 us -> 24.8 us
    pallas_call x1, Pallas kernels: 26 us -> 24.8 us  [shards(): pl.pallas_call(functools.partial(kernel, groups), out_shape=vmem((8, cell...]
where the time goes in v4:
time: 26.7 us; the launch traced here: 26.6 us
  Pallas kernels  24.8 us (93%)
  local copies, waits for them, and re-layouts  1.13 us (4%)
  between operations  0.64 us (2%)
    pallas_call x1, Pallas kernels, shards(): pl.pallas_call(functools.partial(kernel, groups), out_shape=vmem((8, cell...  24.8 us
    unnamed x1, local copies, waits for them, and re-layouts  0.61 us

profile of v4, /device:TPU:8, one launch (start us, length us, event | category | flops | bytes accessed | tf_op | source)
XLA Modules:
  0.0 26.6 jit_solution(156220072630713877)
XLA Ops:
  0.6 24.8 %shard_map.86 = f32[8,1024]{1,0:T(8,128)S(1)} custom-call(f32[6,1024]{1,0:T(8,128)} %adj_h.1, f32[6,1024]{1,0:T(8,128)} %grad_h.1, f32[6,1024]{1,0:T(8,128)} %pre_h.1, bf16[5,6,6,1024]{3,2,1,0:T(8,128)(2,1)} %band_h.1, bf16[512,768]{1,0:T(8,128)(2,1)} %jac_h.1, s32[1,512]{1,0:T(1,128)} %bitcast.4, s32[1,512]{1,0:T(1,128)} %bitcast.5), custom_call_target="tpu_custom_call" | custom-call | tf_op jit(solution)/shard_map/pallas_call | solution.py:442
  25.5 0.5 %slice.7 = f32[1,128]{1,0:T(1,128)} slice(f32[8,1024]{1,0:T(8,128)S(1)} %shard_map.86), slice={[6:7], [0:128]} | slice | bytes 1024 | tf_op jit(solution)/shard_map/slice | solution.py:499
  26.0 0.6 %copy.10 = f32[6,1024]{1,0:T(8,128)} copy(f32[6,1024]{1,0:T(8,128)S(1)} %bitcast.3) | data formatting | bytes 49152

commit v5 on v4

--- a/solution.py
+++ b/solution.py
@@ -88,6 +88,7 @@
     in_sem,
     halo_send,
     halo_recv,
+    told,
     psi_send,
     psi_recv,
     req_send,
@@ -253,6 +254,10 @@
     for dy in (4, 3, 5, 2, 6, 1, 7):
         i = SLOT[dy]
         send(req_s.at[i], req_r.at[i], req_send, req_recv, ahead[X * dy])
+    for dx in (2, 1, 3):
+        pl.semaphore_signal(
+            told, inc=1, device_id=(g, ahead[dx]), device_id_type=MESH
+        )
 
     pick = jnp.broadcast_to(rank, (8, faces)) + jnp.where(
         lax.broadcasted_iota(jnp.int32, (8, faces), 0) < 3, 0, CAP
@@ -266,6 +271,65 @@
     end_place = jnp.where(at_start, local + HALO, local - (cells - HALO))
     takes_end = lax.broadcasted_iota(jnp.int32, (16, faces), 0) == end_place
     reads_end = at_start | at_end
+
+    low8 = lax.broadcasted_iota(jnp.int32, (8, LANES), 1) < CAP
+    low1 = low8[:1]
+
+    def row_values(ref):
+        parts = [ref[:, c * LANES : (c + 1) * LANES] for c in range(tiles)]
+        size = 8 - NVAR
+        for start in range(0, tiles, NVAR // size):
+            some = [p[NVAR:] for p in parts[start : start + NVAR // size]]
+            parts.append(jnp.concatenate(some + some[:1], axis=0))
+        return parts
+
+    def answers(values, wish, other):
+        chunk = jnp.where(low1, wish, pltpu.roll(other, CAP, 1))
+        place_in = jnp.where(low1, pltpu.roll(wish, CAP, 1), other)
+        chunk = jnp.broadcast_to(chunk, (8, LANES))
+        place_in = jnp.broadcast_to(place_in, (8, LANES))
+        found = take_lanes(values[0], place_in)
+        for c in range(1, blocks):
+            found = jnp.where(chunk == c, take_lanes(values[c], place_in), found)
+        turned = pltpu.roll(found, 5, 0)
+        return (
+            jnp.where(low8, found, pltpu.roll(turned, CAP, 1))[:3],
+            jnp.where(low8, pltpu.roll(found, CAP, 1), turned)[:3],
+        )
+
+    pairs = ((4, 3), (5, 2), (6, 1), (7, 0))
+
+    def answer(values, dx, pair):
+        a, b = pair
+        wish = req_r[SLOT[a], dx : dx + 1]
+        other = req_r[SLOT[b], dx : dx + 1] if b else req_own[dx : dx + 1]
+        one, two = answers(values, wish, other)
+        resp_s[SLOT[a], 3 * dx : 3 * dx + 3] = one
+        if b:
+            resp_s[SLOT[b], 3 * dx : 3 * dx + 3] = two
+        else:
+            resp_own[3 * dx : 3 * dx + 3] = two
+
+    def answer_all():
+        wait_all(psi_r, 1, X - 1, psi_recv)
+        wait_all(req_r, 0, Y - 1, req_recv)
+        values = [row_values(psi_s)] + [row_values(psi_r.at[dx]) for dx in range(1, X)]
+        for pair in pairs:
+            for dx in range(X):
+                answer(values[dx], dx, pair)
+            for dy in pair:
+                if dy:
+                    i = SLOT[dy]
+                    send(
+                        resp_s.at[i],
+                        resp_r.at[i],
+                        resp_send,
+                        resp_recv.at[0 if dy in NEAR else 1],
+                        ahead[X * (Y - dy)],
+                    )
+
+    waits = place == (Y // 2) * X - 1
+    pl.when(waits)(answer_all)
 
     pl.when(jnp.logical_not(first))(halo_copies[0].wait_recv)
     pl.when(jnp.logical_not(last))(halo_copies[1].wait_recv)
@@ -302,7 +366,7 @@
     row = jnp.sum(jnp.where(lane // 16 == which, row, 0.0), axis=0, keepdims=True)
     ends_s[...] = row
     ends_r[0] = row
-    wait_all(psi_r, 1, X - 1, psi_recv)
+    pl.semaphore_wait(told, X - 1)
     for s in FAR_FIRST:
         back = (Y - s // X) % Y * X + (X - s % X) % X
         send(ends_s, ends_r.at[back], ends_send, ends_recv, ahead[s])
@@ -310,59 +374,7 @@
         out_o[:NVAR, c * LANES : (c + 1) * LANES] = psi[c]
     out_o[NVAR:, :] = jnp.zeros((8 - NVAR, cells), jnp.float32)
 
-    low8 = lax.broadcasted_iota(jnp.int32, (8, LANES), 1) < CAP
-    low1 = low8[:1]
-
-    def row_values(ref):
-        parts = [ref[:, c * LANES : (c + 1) * LANES] for c in range(tiles)]
-        size = 8 - NVAR
-        for start in range(0, tiles, NVAR // size):
-            some = [p[NVAR:] for p in parts[start : start + NVAR // size]]
-            parts.append(jnp.concatenate(some + some[:1], axis=0))
-        return parts
-
-    def answers(values, wish, other):
-        chunk = jnp.where(low1, wish, pltpu.roll(other, CAP, 1))
-        place_in = jnp.where(low1, pltpu.roll(wish, CAP, 1), other)
-        chunk = jnp.broadcast_to(chunk, (8, LANES))
-        place_in = jnp.broadcast_to(place_in, (8, LANES))
-        found = take_lanes(values[0], place_in)
-        for c in range(1, blocks):
-            found = jnp.where(chunk == c, take_lanes(values[c], place_in), found)
-        turned = pltpu.roll(found, 5, 0)
-        return (
-            jnp.where(low8, found, pltpu.roll(turned, CAP, 1))[:3],
-            jnp.where(low8, pltpu.roll(found, CAP, 1), turned)[:3],
-        )
-
-    pairs = ((4, 3), (5, 2), (6, 1), (7, 0))
-
-    def answer(values, dx, pair):
-        a, b = pair
-        wish = req_r[SLOT[a], dx : dx + 1]
-        other = req_r[SLOT[b], dx : dx + 1] if b else req_own[dx : dx + 1]
-        one, two = answers(values, wish, other)
-        resp_s[SLOT[a], 3 * dx : 3 * dx + 3] = one
-        if b:
-            resp_s[SLOT[b], 3 * dx : 3 * dx + 3] = two
-        else:
-            resp_own[3 * dx : 3 * dx + 3] = two
-
-    wait_all(req_r, 0, Y - 1, req_recv)
-    values = [row_values(psi_s)] + [row_values(psi_r.at[dx]) for dx in range(1, X)]
-    for pair in pairs:
-        for dx in range(X):
-            answer(values[dx], dx, pair)
-        for dy in pair:
-            if dy:
-                i = SLOT[dy]
-                send(
-                    resp_s.at[i],
-                    resp_r.at[i],
-                    resp_send,
-                    resp_recv.at[0 if dy in NEAR else 1],
-                    ahead[X * (Y - dy)],
-                )
+    pl.when(jnp.logical_not(waits))(answer_all)
 
     found = [jnp.zeros((8, LANES), jnp.float32)] * (faces // LANES)
 
@@ -473,6 +485,7 @@
                 dma((7,)),
                 dma((2,)),
                 dma((2,)),
+                pltpu.SemaphoreType.REGULAR,
                 dma,
                 dma,
                 dma,

time: 26.7 us -> 26.1 us (0.978)
  Pallas kernels: 24.8 us -> 24.2 us
    pallas_call x1, Pallas kernels: 24.8 us -> 24.2 us  [shards(): pl.pallas_call(functools.partial(kernel, groups), out_shape=vmem((8, cell...]
where the time goes in v5:
time: 26.1 us; the launch traced here: 26 us
  Pallas kernels  24.2 us (93%)
  local copies, waits for them, and re-layouts  1.13 us (4%)
  between operations  0.64 us (2%)
    pallas_call x1, Pallas kernels, shards(): pl.pallas_call(functools.partial(kernel, groups), out_shape=vmem((8, cell...  24.2 us
    unnamed x1, local copies, waits for them, and re-layouts  0.61 us

profile of v5, /device:TPU:8, one launch (start us, length us, event | category | flops | bytes accessed | tf_op | source)
XLA Modules:
  0.0 26.0 jit_solution(11427758645019684070)
XLA Ops:
  0.6 24.2 %shard_map.86 = f32[8,1024]{1,0:T(8,128)S(1)} custom-call(f32[6,1024]{1,0:T(8,128)} %adj_h.1, f32[6,1024]{1,0:T(8,128)} %grad_h.1, f32[6,1024]{1,0:T(8,128)} %pre_h.1, bf16[5,6,6,1024]{3,2,1,0:T(8,128)(2,1)} %band_h.1, bf16[512,768]{1,0:T(8,128)(2,1)} %jac_h.1, s32[1,512]{1,0:T(1,128)} %bitcast.4, s32[1,512]{1,0:T(1,128)} %bitcast.5), custom_call_target="tpu_custom_call" | custom-call | tf_op jit(solution)/shard_map/pallas_call | solution.py:454
  24.9 0.5 %slice.7 = f32[1,128]{1,0:T(1,128)} slice(f32[8,1024]{1,0:T(8,128)S(1)} %shard_map.86), slice={[6:7], [0:128]} | slice | bytes 1024 | tf_op jit(solution)/shard_map/slice | solution.py:512
  25.4 0.6 %copy.10 = f32[6,1024]{1,0:T(8,128)} copy(f32[6,1024]{1,0:T(8,128)S(1)} %bitcast.3) | data formatting | bytes 49152

commit v6 on v5

--- a/solution.py
+++ b/solution.py
@@ -60,13 +60,10 @@
     cell_h,
     box_h,
     out_o,
-    adj_v,
-    grad_v,
-    pre_v,
+    state_v,
     band_v,
     jac_v,
-    cell_v,
-    box_v,
+    face_v,
     bandf,
     band_edge,
     shf,
@@ -85,19 +82,16 @@
     ends_r,
     part_s,
     part_r,
+    count_v,
     in_sem,
-    halo_send,
+    sent,
     halo_recv,
     told,
-    psi_send,
     psi_recv,
-    req_send,
     req_recv,
     resp_send,
     resp_recv,
-    ends_send,
     ends_recv,
-    part_send,
     part_recv,
 ):
     cells = adj_h.shape[1]
@@ -121,16 +115,14 @@
 
     loads = [
         pltpu.make_async_copy(src, dst, in_sem.at[i])
-        for i, (src, dst) in enumerate(
-            (
-                (band_h, band_v),
-                (adj_h, adj_v),
-                (grad_h, grad_v),
-                (pre_h, pre_v),
-                (cell_h, cell_v),
-                (box_h, box_v),
-                (jac_h, jac_v),
-            )
+        for src, dst, i in (
+            (band_h, band_v, 0),
+            (adj_h, state_v.at[0], 1),
+            (grad_h, state_v.at[1], 1),
+            (pre_h, state_v.at[2], 1),
+            (cell_h, face_v.at[0], 2),
+            (box_h, face_v.at[1], 2),
+            (jac_h, jac_v, 3),
         )
     ]
     for load in loads:
@@ -156,24 +148,34 @@
         tile = band_v[t // NVAR, t % NVAR].astype(jnp.float32)
         bandf[t] = tile
         start, end = tile[:, :LANES], tile[:, cells - LANES :]
+        turned = pltpu.roll(jnp.where(head, start, end), CAP, 1)
         band_edge[t, :, :LANES] = end
-        band_edge[t, :, 2 * LANES :] = start
+        band_edge[t, :, LANES:] = turned
         u = t % half
-        ends = pltpu.roll(jnp.where(head, start, end), 8 * u + 4, 1)
-        packed[t // half] = jnp.where(lane // 8 == u, ends, packed[t // half])
+        ends = jnp.where(lane < 32, start, turned)
+        ends = pltpu.roll(ends, 4 * u, 1) if u else ends
+        own_lanes = (lane // 4 == u) | (lane // 4 == half + u)
+        packed[t // half] = jnp.where(own_lanes, ends, packed[t // half])
     rest = jnp.zeros((8 - NVAR, LANES), jnp.float32)
     halo_s[0] = jnp.concatenate([packed[0], rest], axis=0)
     halo_s[1] = jnp.concatenate([packed[1], rest], axis=0)
-    for load in loads[1:4]:
-        load.wait()
-    adj, grad, pre = adj_v[...], grad_v[...], pre_v[...]
+    pltpu.make_async_copy(state_v, state_v, in_sem.at[1]).wait()
+    adj, grad, pre = state_v[0], state_v[1], state_v[2]
+    turned = [
+        pltpu.roll(jnp.where(head, v[:, :LANES], v[:, cells - LANES :]), CAP, 1)
+        for v in (adj, grad, pre)
+    ]
     ends = [
-        jnp.where(head, v[:, :LANES], v[:, cells - LANES :]) for v in (adj, grad, pre)
+        jnp.where(lane < 32, v[:, :LANES], t) for v, t in zip((adj, grad, pre), turned)
     ]
     packed = jnp.where(
-        (lane < 16) | (lane >= 112),
+        (lane < 16) | ((lane >= 48) & (lane < 72)),
         ends[0],
-        jnp.where(head, pltpu.roll(ends[1], 32, 1), pltpu.roll(ends[2], 80, 1)),
+        jnp.where(
+            (lane < 32) | ((lane >= 72) & (lane < 88)),
+            pltpu.roll(ends[1], 16, 1),
+            pltpu.roll(ends[2], 32, 1),
+        ),
     )
     halo_s[2] = jnp.concatenate([packed, rest], axis=0)
 
@@ -185,8 +187,8 @@
     def _():
         halo_r[...] = jnp.zeros_like(halo_r)
 
-    loads[4].wait()
-    cell = cell_v[...]
+    pltpu.make_async_copy(face_v, face_v, in_sem.at[2]).wait()
+    cell = face_v[0]
     owner, local = cell // cells, cell % cells
     far = ((owner // X - y + Y) % Y) * X + (owner % X - x + X) % X
     slots = lax.broadcasted_iota(jnp.int32, (dom_count, faces), 0)
@@ -239,7 +241,7 @@
             pltpu.make_async_remote_copy(
                 src_ref=halo_s,
                 dst_ref=landing,
-                send_sem=halo_send.at[i],
+                send_sem=sent,
                 recv_sem=halo_recv.at[i],
                 device_id=target,
                 device_id_type=MESH,
@@ -250,10 +252,10 @@
 
     for dx in (2, 1, 3):
         i = X - dx
-        send(psi_s, psi_r.at[i], psi_send, psi_recv, ahead[dx])
+        send(psi_s, psi_r.at[i], sent, psi_recv, ahead[dx])
     for dy in (4, 3, 5, 2, 6, 1, 7):
         i = SLOT[dy]
-        send(req_s.at[i], req_r.at[i], req_send, req_recv, ahead[X * dy])
+        send(req_s.at[i], req_r.at[i], sent, req_recv, ahead[X * dy])
     for dx in (2, 1, 3):
         pl.semaphore_signal(
             told, inc=1, device_id=(g, ahead[dx]), device_id_type=MESH
@@ -263,8 +265,7 @@
         lax.broadcasted_iota(jnp.int32, (8, faces), 0) < 3, 0, CAP
     )
     far8 = jnp.broadcast_to(far, (8, faces))
-    loads[5].wait()
-    box = box_v[...]
+    box = face_v[1]
     box_far = ((box // X - y + Y) % Y) * X + (box % X - x + X) % X
     feeds = slots == box_far
     at_start, at_end = local < HALO, local >= cells - HALO
@@ -335,28 +336,22 @@
     pl.when(jnp.logical_not(last))(halo_copies[1].wait_recv)
     left = halo_l[:, :NVAR, :]
     right = halo_r[:, :NVAR, :]
-    from_left = lane % 8 < 4
     for h in range(2):
-        both = jnp.where(from_left, left[h], right[h])
+        both = jnp.where(lane < 4 * half, right[h], left[h])
         for u in range(half):
-            band_edge[h * half + u, :, LANES : 2 * LANES] = pltpu.roll(
-                both, LANES - (8 * u + 4), 1
-            )
-
-    def edge(v, turn):
-        between = jnp.where(head, right[2], left[2])
-        if turn:
-            between = jnp.where(
-                head, pltpu.roll(right[2], turn, 1), pltpu.roll(left[2], turn, 1)
-            )
-        return jnp.concatenate(
-            [v[:, cells - LANES :], between, v[:, :LANES]], axis=1
-        )
+            back = pltpu.roll(both, LANES - 4 * u, 1) if u else both
+            band_edge[h * half + u, :, LANES : LANES + CAP] = back[:, :CAP]
+    both = jnp.where(lane < 48, right[2], left[2])
+
+    def edge(i, v):
+        back = pltpu.roll(both, LANES - 16 * i, 1) if i else both
+        middle = jnp.where(head, back, turned[i])
+        return jnp.concatenate([v[:, cells - LANES :], middle], axis=1)
 
     outer = sweep(
-        edge(adj, 0), edge(grad, 96), edge(pre, 48), band_edge, shf, 3 * LANES
+        edge(0, adj), edge(1, grad), edge(2, pre), band_edge, shf, 2 * LANES
     )
-    psi[0] = jnp.where(head, outer[:, 2 * LANES :], psi[0])
+    psi[0] = jnp.where(lane < 32, pltpu.roll(outer[:, LANES:], CAP, 1), psi[0])
     psi[-1] = jnp.where(head, psi[-1], outer[:, :LANES])
     ends = jnp.where(head, psi[0], psi[-1])
     row = jnp.zeros((NVAR, LANES), jnp.float32)
@@ -369,7 +364,7 @@
     pl.semaphore_wait(told, X - 1)
     for s in FAR_FIRST:
         back = (Y - s // X) % Y * X + (X - s % X) % X
-        send(ends_s, ends_r.at[back], ends_send, ends_recv, ahead[s])
+        send(ends_s, ends_r.at[back], sent, ends_recv, ahead[s])
     for c in range(blocks):
         out_o[:NVAR, c * LANES : (c + 1) * LANES] = psi[c]
     out_o[NVAR:, :] = jnp.zeros((8 - NVAR, cells), jnp.float32)
@@ -428,16 +423,14 @@
         part_s[s] = sums[s : s + 1]
     part_r[0] = sums[0:1]
     for s in FAR_FIRST:
-        send(part_s.at[s], part_r.at[s], part_send, part_recv, ahead[s])
+        send(part_s.at[s], part_r.at[s], sent, part_recv, ahead[s])
     wait_all(part_r, 1, dom_count - 1, part_recv)
     out_o[NVAR : NVAR + 1, :SENS] = jnp.sum(part_r[...], axis=0)
-    pl.when(jnp.logical_not(last))(halo_copies[0].wait_send)
-    pl.when(jnp.logical_not(first))(halo_copies[1].wait_send)
-    wait_all(req_s, 0, Y - 1, req_send)
-    wait_all(psi_r, 1, X - 1, psi_send)
     wait_all(resp_s, 0, Y - 1, resp_send)
-    wait_all(ends_r, 1, dom_count - 1, ends_send)
-    wait_all(part_s, 1, dom_count - 1, part_send)
+    left_rows = X * (Y - 1) + (X - 1) * 8 * tiles + 2 * (dom_count - 1)
+    one_halo = jnp.logical_or(first, last)
+    pl.when(one_halo)(lambda: wait_all(count_v, 0, left_rows + 24, sent))
+    pl.when(jnp.logical_not(one_halo))(lambda: wait_all(count_v, 0, left_rows + 48, sent))
 
 
 def solution(mesh):
@@ -457,15 +450,12 @@
             in_specs=[pl.BlockSpec(memory_space=pl.ANY)] * 7,
             out_specs=pl.BlockSpec(memory_space=pltpu.VMEM),
             scratch_shapes=[
-                vmem((NVAR, cells), f32),
-                vmem((NVAR, cells), f32),
-                vmem((NVAR, cells), f32),
+                vmem((3, NVAR, cells), f32),
                 vmem((BAND, NVAR, NVAR, cells), jnp.bfloat16),
                 vmem((faces, NVAR * SENS), jnp.bfloat16),
-                vmem((1, faces), jnp.int32),
-                vmem((1, faces), jnp.int32),
+                vmem((2, 1, faces), jnp.int32),
                 vmem((BAND * NVAR, NVAR, cells), f32),
-                vmem((BAND * NVAR, NVAR, 3 * LANES), f32),
+                vmem((BAND * NVAR, NVAR, 2 * LANES), f32),
                 vmem((BAND, NVAR, cells), f32),
                 vmem((3, 8, LANES), f32),
                 vmem((3, 8, LANES), f32),
@@ -482,18 +472,15 @@
                 vmem((dom_count, 1, LANES), f32),
                 vmem((dom_count, 1, LANES), f32),
                 vmem((dom_count, 1, LANES), f32),
-                dma((7,)),
-                dma((2,)),
+                vmem((X * (Y - 1) + 3 * packed * 8 // LANES + 2 * dom_count + 46, 1, LANES), f32),
+                dma((4,)),
+                dma,
                 dma((2,)),
                 pltpu.SemaphoreType.REGULAR,
                 dma,
                 dma,
                 dma,
-                dma,
-                dma,
                 dma((2,)),
-                dma,
-                dma,
                 dma,
                 dma,
             ],

time: 26.1 us -> 26.1 us (level)
  no operation moved by 1% of the time
where the time goes in v6:
time: 26.1 us; the launch traced here: 26 us
  Pallas kernels  24.2 us (93%)
  local copies, waits for them, and re-layouts  1.13 us (4%)
  between operations  0.64 us (2%)
    pallas_call x1, Pallas kernels, shards(): pl.pallas_call(functools.partial(kernel, groups), out_shape=vmem((8, cell...  24.2 us
    unnamed x1, local copies, waits for them, and re-layouts  0.61 us

profile of v6, /device:TPU:8, one launch (start us, length us, event | category | flops | bytes accessed | tf_op | source)
XLA Modules:
  0.0 26.0 jit_solution(1923862239906295357)
XLA Ops:
  0.6 24.2 %shard_map.86 = f32[8,1024]{1,0:T(8,128)S(1)} custom-call(f32[6,1024]{1,0:T(8,128)} %adj_h.1, f32[6,1024]{1,0:T(8,128)} %grad_h.1, f32[6,1024]{1,0:T(8,128)} %pre_h.1, bf16[5,6,6,1024]{3,2,1,0:T(8,128)(2,1)} %band_h.1, bf16[512,768]{1,0:T(8,128)(2,1)} %jac_h.1, s32[1,512]{1,0:T(1,128)} %bitcast.4, s32[1,512]{1,0:T(1,128)} %bitcast.5), custom_call_target="tpu_custom_call" | custom-call | tf_op jit(solution)/shard_map/pallas_call | solution.py:447
  24.9 0.5 %slice.7 = f32[1,128]{1,0:T(1,128)} slice(f32[8,1024]{1,0:T(8,128)S(1)} %shard_map.86), slice={[6:7], [0:128]} | slice | bytes 1024 | tf_op jit(solution)/shard_map/slice | solution.py:499
  25.4 0.6 %copy.10 = f32[6,1024]{1,0:T(8,128)} copy(f32[6,1024]{1,0:T(8,128)S(1)} %bitcast.3) | data formatting | bytes 49152

commit v7 on v6

--- a/solution.py
+++ b/solution.py
@@ -60,6 +60,7 @@
     cell_h,
     box_h,
     out_o,
+    zero_o,
     state_v,
     band_v,
     jac_v,
@@ -368,6 +369,7 @@
     for c in range(blocks):
         out_o[:NVAR, c * LANES : (c + 1) * LANES] = psi[c]
     out_o[NVAR:, :] = jnp.zeros((8 - NVAR, cells), jnp.float32)
+    zero_o[...] = jnp.zeros_like(zero_o)
 
     pl.when(jnp.logical_not(waits))(answer_all)
 
@@ -444,11 +446,11 @@
         f32 = jnp.float32
         vmem = pltpu.VMEM
         dma = pltpu.SemaphoreType.DMA
-        out = pl.pallas_call(
+        out, zero = pl.pallas_call(
             functools.partial(kernel, groups),
-            out_shape=vmem((8, cells), f32),
+            out_shape=(vmem((8, cells), f32), vmem((1, cells), f32)),
             in_specs=[pl.BlockSpec(memory_space=pl.ANY)] * 7,
-            out_specs=pl.BlockSpec(memory_space=pltpu.VMEM),
+            out_specs=[pl.BlockSpec(memory_space=pltpu.VMEM)] * 2,
             scratch_shapes=[
                 vmem((3, NVAR, cells), f32),
                 vmem((BAND, NVAR, NVAR, cells), jnp.bfloat16),
@@ -496,7 +498,9 @@
             face_cell.reshape(1, faces),
             face_box.reshape(1, faces),
         )
-        return out[:NVAR], out[NVAR : NVAR + 1, :SENS]
+        state = lax.optimization_barrier(out[:NVAR] + zero)
+        zero = zero[:, :SENS] * state[:1, :SENS]
+        return state, out[NVAR : NVAR + 1, :SENS] + zero
 
     return jax.shard_map(
         shards,

time: 26.1 us -> 25.6 us (0.981)
  local copies, waits for them, and re-layouts: 1.13 us -> 0.09 us
  other arithmetic: 0 us -> 0.53 us
    add x0 -> x2, other arithmetic: none -> 0.53 us  [the longest x1 0.52 us: shards(): return (state, out[NVAR:NVAR + 1, :SENS] + zero)]
    unnamed x1 -> x2, local copies, waits for them, and re-layouts: 0.61 us -> 0.09 us
    slice x1 -> x0, local copies, waits for them, and re-layouts: 0.51 us -> none  [shards(): return (out[:NVAR], out[NVAR:NVAR + 1, :SENS])]
where the time goes in v7:
time: 25.6 us; the launch traced here: 25.5 us
  Pallas kernels  24.2 us (95%)
  between operations  0.66 us (3%)
  other arithmetic  0.53 us (2%)
    pallas_call x1, Pallas kernels, shards(): pl.pallas_call(functools.partial(kernel, groups), out_shape=(vmem((8, cel...  24.2 us
    add x1, other arithmetic, shards(): return (state, out[NVAR:NVAR + 1, :SENS] + zero)  0.52 us

profile of v7, /device:TPU:8, one launch (start us, length us, event | category | flops | bytes accessed | tf_op | source)
XLA Modules:
  0.0 25.5 jit_solution(13625129124086016078)
XLA Ops:
  0.6 24.2 %shard_map.86 = (f32[8,1024]{1,0:T(8,128)S(1)}, f32[1,1024]{1,0:T(1,128)S(1)}) custom-call(f32[6,1024]{1,0:T(8,128)} %adj_h.1, f32[6,1024]{1,0:T(8,128)} %grad_h.1, f32[6,1024]{1,0:T(8,128)} %pre_h.1, bf16[5,6,6,1024]{3,2,1,0:T(8,128)(2,1)} %band_h.1, bf16[512,768]{1,0:T(8,128)(2,1)} %jac_h.1, s32[1,512]{1,0:T(1,128)} %bitcast.4, s32[1,512]{1,0:T(1,128)} %bitcast.5), custom_call_target="tpu_custom_call" | custom-call | tf_op jit(solution)/shard_map/pallas_call | solution.py:449
  24.9 0.0 copy-start
  24.9 0.5 %fusion = f32[1,128]{1,0:T(1,128)} fusion(f32[6,1024]{1,0:T(8,128)S(1)} %slice_add_fusion, f32[1,1024]{1,0:T(1,128)S(1)} %get-tuple-element.5, f32[8,1024]{1,0:T(8,128)S(1)} %get-tuple-element.4), kind=kLoop, calls=%fused_computation.2 | loop fusion | flops 256 | bytes 2048 | tf_op jit(solution)/shard_map/add | solution.py:503
  25.4 0.1 copy-done
  (1 shorter events, 0.0 us)
Async XLA Ops:
  24.9 0.6 %copy-start = (f32[6,1024]{1,0:T(8,128)}, f32[6,1024]{1,0:T(8,128)S(1)}, u32[]{:S(2)}) copy-start(f32[6,1024]{1,0:T(8,128)S(1)} %slice_add_fusion) | copy-start | bytes 73732

commit v8 on v7

--- a/solution.py
+++ b/solution.py
@@ -251,12 +251,12 @@
     pl.when(jnp.logical_not(last))(halo_copies[0].start)
     pl.when(jnp.logical_not(first))(halo_copies[1].start)
 
+    for dy in (4, 3, 5, 2, 6, 1, 7):
+        i = SLOT[dy]
+        send(req_s.at[i], req_r.at[i], sent, req_recv, ahead[X * dy])
     for dx in (2, 1, 3):
         i = X - dx
         send(psi_s, psi_r.at[i], sent, psi_recv, ahead[dx])
-    for dy in (4, 3, 5, 2, 6, 1, 7):
-        i = SLOT[dy]
-        send(req_s.at[i], req_r.at[i], sent, req_recv, ahead[X * dy])
     for dx in (2, 1, 3):
         pl.semaphore_signal(
             told, inc=1, device_id=(g, ahead[dx]), device_id_type=MESH

time: 25.6 us -> 25.6 us (level)
  no operation moved by 1% of the time
where the time goes in v8:
time: 25.6 us; the launch traced here: 25.5 us
  Pallas kernels  24.2 us (95%)
  between operations  0.66 us (3%)
  other arithmetic  0.53 us (2%)
    pallas_call x1, Pallas kernels, shards(): pl.pallas_call(functools.partial(kernel, groups), out_shape=(vmem((8, cel...  24.2 us
    add x1, other arithmetic, shards(): return (state, out[NVAR:NVAR + 1, :SENS] + zero)  0.52 us

profile of v8, /device:TPU:8, one launch (start us, length us, event | category | flops | bytes accessed | tf_op | source)
XLA Modules:
  0.0 25.5 jit_solution(5508839789012280623)
XLA Ops:
  0.6 24.2 %shard_map.86 = (f32[8,1024]{1,0:T(8,128)S(1)}, f32[1,1024]{1,0:T(1,128)S(1)}) custom-call(f32[6,1024]{1,0:T(8,128)} %adj_h.1, f32[6,1024]{1,0:T(8,128)} %grad_h.1, f32[6,1024]{1,0:T(8,128)} %pre_h.1, bf16[5,6,6,1024]{3,2,1,0:T(8,128)(2,1)} %band_h.1, bf16[512,768]{1,0:T(8,128)(2,1)} %jac_h.1, s32[1,512]{1,0:T(1,128)} %bitcast.4, s32[1,512]{1,0:T(1,128)} %bitcast.5), custom_call_target="tpu_custom_call" | custom-call | tf_op jit(solution)/shard_map/pallas_call | solution.py:449
  24.9 0.0 copy-start
  24.9 0.5 %fusion = f32[1,128]{1,0:T(1,128)} fusion(f32[6,1024]{1,0:T(8,128)S(1)} %slice_add_fusion, f32[1,1024]{1,0:T(1,128)S(1)} %get-tuple-element.5, f32[8,1024]{1,0:T(8,128)S(1)} %get-tuple-element.4), kind=kLoop, calls=%fused_computation.2 | loop fusion | flops 256 | bytes 2048 | tf_op jit(solution)/shard_map/add | solution.py:503
  25.4 0.1 copy-done
  (1 shorter events, 0.0 us)
Async XLA Ops:
  24.9 0.6 %copy-start = (f32[6,1024]{1,0:T(8,128)}, f32[6,1024]{1,0:T(8,128)S(1)}, u32[]{:S(2)}) copy-start(f32[6,1024]{1,0:T(8,128)S(1)} %slice_add_fusion) | copy-start | bytes 73732
